TPU v7x, 32 devices: a whole 2x2x4 slice. The times are simulated.
32 devices in a mesh: tm: 2 (over y), height: 16 (over z, x, core).
Axes of the slice: x: 2, y: 2, z: 4, core: 2. Of those that a mesh axis runs over, the one named last changes fastest.
Arguments:
- latents: bfloat16 [2, 4, 32, 128, 512], P(None, 'tm', 'height'), may hold values from -6 to 6
- norm_gain: float32 [512], replicated, may hold values from 0.25 to 1.75
- spatial_weight: bfloat16 [3, 3, 512, 512], replicated, may hold values from -0.09375 to 0.09375
- temporal_weight: float32 [3, 512], replicated, may hold values from -3 to 3
- codebooks: bfloat16 [2, 32768, 512], P(None, 'height'), may hold values from -6 to 6
- ema_counts: float32 [2, 32768], P(None, 'height'), may hold values from 0.3 to 30
- ema_sums: float32 [2, 32768, 512], P(None, 'height', 'tm'), may hold values from -6 to 6
- decay: float32 [2], replicated, may hold values from 0.6 to 0.9
- codes_first: int32 [2, 4, 32, 128], P(None, 'tm', 'height'), may hold values from 0 to 32767, as said below
- codes_second: int32 [2, 4, 32, 128], P(None, 'tm', 'height'), may hold values from 0 to 32767, as said below
Outputs:
- ema_counts_new: float32 [2, 32768], P(None, 'height')
- ema_sums_new: float32 [2, 32768, 512], P(None, 'height', 'tm')
- error: float32 [2, 4, 32, 128], P(None, 'tm', 'height')
Inputs may be any that keep to these rules, and one draw needn't show every extreme that they name: `codes_first`: the codes of index o of height are o * 2048 to (o + 1) * 2048 - 1. In the latents of one device (all 2 clips over its 2 frames and 2 rows) at most 128 name codes of one owner o, and in every draw, for every index of tm, some owner gets exactly 128 from every device of that index. `codes_second`: as for codes_first, drawn independently.
All inputs are finite; a program needn't handle non-finite values.
Results may differ from a plain program's by a relative error of at most 0.0031.
Values may be sent and summed in bfloat16 or wider, within the bound.
A program may use at most 128 MiB of HBM per device.

v0:
```python
import jax
import jax.numpy as jnp
from jax import lax
from jax.experimental import pallas as pl
from jax.experimental.pallas import tpu as pltpu
from jax.sharding import PartitionSpec as P


def normalize(values, norm_gain):
    widened = values.astype(jnp.float32)
    inverse = lax.rsqrt(jnp.mean(widened * widened, axis=-1, keepdims=True) + 1e-06)
    return (widened * inverse * norm_gain).astype(jnp.bfloat16)


def convolve(padded, kernel):
    clips, frames, rows, width, channels = padded.shape
    summed = lax.conv_general_dilated(
        padded.reshape(clips * frames, rows, width, channels),
        kernel,
        (1, 1),
        ((0, 0), (1, 1)),
        dimension_numbers=("NHWC", "HWIO", "NHWC"),
        preferred_element_type=jnp.float32,
    )
    hidden = jax.nn.silu(summed).astype(jnp.bfloat16)
    return hidden.reshape(clips, frames, rows - 2, width, channels)


def slots_of(indices, num_peers, capacity, code_rows):
    amount = indices.shape[1]
    owners = indices // code_rows
    markers = (owners[:, :, None] == jnp.arange(num_peers, dtype=jnp.int32)).astype(jnp.bfloat16)
    steps = jnp.arange(amount, dtype=jnp.int32)
    earlier = (steps[:, None] > steps[None, :]).astype(jnp.bfloat16)
    before = jnp.einsum("ij,sjp->isp", earlier, markers, preferred_element_type=jnp.float32)
    ranking = jnp.sum(before.swapaxes(0, 1) * markers.astype(jnp.float32), axis=2)
    return owners * capacity + ranking.astype(jnp.int32)


def wanted_of(indices, slot_ids, total):
    match = slot_ids[:, None, :] == jnp.arange(total, dtype=jnp.int32)[None, :, None]
    return jnp.sum(jnp.where(match, indices[:, None, :] + 1, 0), axis=2) - 1


def block_of(count, limit):
    block = count
    while block > limit and block % 2 == 0:
        block //= 2
    return block


def pack(slot_ids, vectors, total, slabs):
    amount, channels = vectors.shape
    part = channels // slabs
    block = block_of(total, 512)

    def kernel(slot_ref, vector_ref, out_ref):
        start = pl.program_id(0) * block
        places = start + lax.broadcasted_iota(jnp.int32, (block, amount), 0)
        hot = jnp.where(places == slot_ref[...], 1.0, 0.0).astype(jnp.bfloat16)
        rows = jnp.dot(hot, vector_ref[...], preferred_element_type=jnp.float32)
        rows = rows.astype(jnp.bfloat16)
        for slab in range(slabs):
            out_ref[slab] = rows[:, slab * part : (slab + 1) * part]

    return pl.pallas_call(
        kernel,
        grid=(total // block,),
        out_shape=jax.ShapeDtypeStruct((slabs, total, part), jnp.bfloat16),
        in_specs=[
            pl.BlockSpec((1, amount), lambda i: (0, 0)),
            pl.BlockSpec((amount, channels), lambda i: (0, 0)),
        ],
        out_specs=pl.BlockSpec((slabs, block, part), lambda i: (0, i, 0)),
        cost_estimate=pl.CostEstimate(
            flops=2 * total * amount * channels, bytes_accessed=6 * total * part * slabs, transcendentals=0
        ),
        name="pack",
    )(slot_ids[None, :], vectors)


def tally(which, ids, vectors, ema_sums, decay, into):
    amount, part = vectors.shape
    code_rows = ema_sums.shape[1]
    block = block_of(code_rows, 256)

    def kernel(decay_ref, id_ref, vector_ref, old_ref, *rest):
        out_ref = rest[-1]
        start = pl.program_id(0) * block
        places = start + lax.broadcasted_iota(jnp.int32, (block, amount), 0)
        hot = jnp.where(places == id_ref[...], 1.0, 0.0).astype(jnp.bfloat16)
        sums = jnp.dot(hot, vector_ref[...], preferred_element_type=jnp.float32)
        keep = decay_ref[which]
        out_ref[0] = keep * old_ref[0] + (1.0 - keep) * sums

    operands = [decay, ids[None, :], vectors, ema_sums]
    in_specs = [
        pl.BlockSpec(memory_space=pltpu.SMEM),
        pl.BlockSpec((1, amount), lambda i: (0, 0)),
        pl.BlockSpec((amount, part), lambda i: (0, 0)),
        pl.BlockSpec((1, block, part), lambda i: (which, i, 0)),
    ]
    aliases = {}
    if into is not None:
        operands.append(into)
        in_specs.append(pl.BlockSpec(memory_space=pl.ANY))
        aliases = {4: 0}
    return pl.pallas_call(
        kernel,
        grid=(code_rows // block,),
        out_shape=jax.ShapeDtypeStruct(ema_sums.shape, jnp.float32),
        in_specs=in_specs,
        out_specs=pl.BlockSpec((1, block, part), lambda i: (which, i, 0)),
        input_output_aliases=aliases,
        cost_estimate=pl.CostEstimate(
            flops=2 * code_rows * amount * part, bytes_accessed=8 * code_rows * part, transcendentals=0
        ),
        name="tally",
    )(*operands)


def rows_by(ids, count):
    return (ids[:, None] == jnp.arange(count, dtype=jnp.int32)[None, :]).astype(jnp.bfloat16)


def picked(ids, table):
    return jnp.dot(
        rows_by(ids, table.shape[0]), table, preferred_element_type=jnp.float32
    ).astype(jnp.bfloat16)


def body(
    latents,
    norm_gain,
    spatial_weight,
    temporal_weight,
    codebooks,
    ema_counts,
    ema_sums,
    decay,
    codes_first,
    codes_second,
):
    frame_count = latents.shape[1]
    channels = latents.shape[-1]
    num_peers = lax.axis_size("height")
    slabs = lax.axis_size("tm")
    part = channels // slabs
    code_rows = codebooks.shape[1]
    amount = codes_first.size
    capacity = 2 * amount // num_peers
    total = num_peers * capacity
    offset = lax.axis_index("height") * code_rows
    slab = lax.axis_index("tm")
    everyone = ("tm", "height")

    peers = [(i, i + 1) for i in range(num_peers - 1)]
    first_row = normalize(latents[:, :, :1], norm_gain)
    last_row = normalize(latents[:, :, -1:], norm_gain)
    codes = jnp.stack([codes_first.reshape(-1), codes_second.reshape(-1)])
    first_row, last_row, codes = lax.optimization_barrier((first_row, last_row, codes))
    row_before = lax.ppermute(last_row, "height", peers)
    row_after = lax.ppermute(first_row, "height", [(j, i) for i, j in peers])

    slots = slots_of(codes, num_peers, capacity, code_rows)
    wanted = wanted_of(codes, slots, total).reshape(2, num_peers, capacity).swapaxes(0, 1)
    wanted = jnp.broadcast_to(wanted[None], (slabs,) + wanted.shape).reshape(
        slabs * num_peers, 2 * capacity
    )
    got = lax.all_to_all(wanted, everyone, split_axis=0, concat_axis=0, tiled=True)
    got = got.reshape(slabs, num_peers, 2, capacity) - offset
    mine = lax.dynamic_index_in_dim(got[:, :, 0], slab, 0, keepdims=False)
    answer = picked(mine.reshape(-1), codebooks[0]).reshape(num_peers, capacity, channels)
    answer = lax.all_to_all(answer, "height", split_axis=0, concat_axis=0, tiled=True)

    widened = latents.astype(jnp.float32)
    normed = normalize(latents, norm_gain)
    padded = jnp.concatenate([row_before, normed, row_after], axis=2)
    hidden = convolve(padded, spatial_weight)
    earlier = lax.ppermute(hidden, "tm", [(i, i + 1) for i in range(slabs - 1)])
    first_ids, second_ids = got[:, :, 0].reshape(-1), got[:, :, 1].reshape(-1)
    table = lax.dynamic_slice_in_dim(codebooks[1], slab * part, part, axis=1)
    second_quant = picked(second_ids, table)
    marks = jnp.arange(code_rows, dtype=jnp.int32)[:, None]
    counts = jnp.stack(
        [
            jnp.sum((marks == ids[None, :]).astype(jnp.float32), axis=1)
            for ids in (first_ids, second_ids)
        ]
    )
    earlier, second_quant = lax.optimization_barrier((earlier, second_quant))
    sequence = jnp.concatenate([earlier, hidden], axis=1)
    mixed = jnp.zeros(latents.shape, jnp.float32)
    for tap in range(3):
        begin = frame_count - 2 + tap
        mixed = mixed + temporal_weight[tap] * sequence[:, begin : begin + frame_count].astype(
            jnp.float32
        )
    encoded = (widened + mixed).astype(jnp.bfloat16)
    flat = encoded.reshape(-1, channels)

    def deliver(vectors, slot):
        packed = pack(slot, vectors, total, slabs).reshape(slabs * num_peers, capacity, part)
        there = lax.all_to_all(packed, everyone, split_axis=0, concat_axis=0, tiled=True)
        return there.reshape(-1, part)

    first_there = deliver(flat, slots[0])
    first_quant = picked(slots[0], answer.reshape(total, channels))
    residual = (flat.astype(jnp.float32) - first_quant.astype(jnp.float32)).astype(jnp.bfloat16)
    second_there = deliver(residual, slots[1])

    leftover = second_there.astype(jnp.float32) - second_quant.astype(jnp.float32)
    squares = jnp.sum(leftover * leftover, axis=-1).reshape(slabs * num_peers, capacity)
    squares = lax.all_to_all(squares, everyone, split_axis=0, concat_axis=0, tiled=True)
    squares = jnp.sum(squares.reshape(slabs, total), axis=0)
    match = slots[1][:, None] == jnp.arange(total, dtype=jnp.int32)[None, :]
    error = jnp.sum(jnp.where(match, squares[None, :], 0.0), axis=1) / channels
    error = error.reshape(codes_first.shape)

    ema_sums_new = tally(0, first_ids, first_there, ema_sums, decay, None)
    ema_sums_new = tally(1, second_ids, second_there, ema_sums, decay, ema_sums_new)
    keep = decay[:, None]
    ema_counts_new = keep * ema_counts + (1.0 - keep) * counts
    return (ema_counts_new, ema_sums_new, error)


def solution(mesh):
    return jax.shard_map(
        body,
        mesh=mesh,
        in_specs=(
            P(None, "tm", "height", None, None),
            P(),
            P(),
            P(),
            P(None, "height", None),
            P(None, "height"),
            P(None, "height", "tm"),
            P(),
            P(None, "tm", "height", None),
            P(None, "tm", "height", None),
        ),
        out_specs=(P(None, "height"), P(None, "height", "tm"), P(None, "tm", "height", None)),
        check_vma=False,
    )
```

profile of v0, /device:TPU:0, one launch (start us, length us, event | category | flops | bytes accessed | tf_op | source)
XLA Modules:
  0.0 211.4 jit_solution(3714193497946576700)
XLA Ops:
  0.6 1.6 fusion.26
  2.2 0.7 pad_add_fusion
  3.0 1.5 fusion.28
  5.1 2.0 select_reduce_fusion
  7.8 7.3 %all-to-all-start = ((s32[32,1,256]{2,1,0:T(1,128)}), s32[32,1,256]{2,1,0:T(1,128)S(1)}, u32[]{:S(2)}, u32[]{:S(2)}) async-start(s32[32,1,256]{2,1,0:T(1,128)} %bitcast.7), calls=%async_computation | async-start | bytes 65536 | tf_op jit(solution)/shard_map/all_to_all | solution.py:170
  15.1 2.2 %collective-permute-start = (bf16[2,2,1,128,512]{4,3,2,1,0:T(8,128)(2,1)S(1)}, bf16[2,2,1,128,512]{4,3,2,1,0:T(8,128)(2,1)S(1)}, u32[]{:S(2)}, u32[]{:S(2)}) collective-permute-start(bf16[2,2,1,128,512]{4,3,2,1,0:T(8,128)(2,1)S(1)} %get-tuple-element.9), channel_id=1, source_target_pairs={{0,1},{1,2},{2,3},{3,4},{4,5},{5,6},{6,7},{7,8},{8,9},{9,10},{10,1... | collective-permute-start | bytes 1572872 | tf_op jit(solution)/shard_map/ppermute | solution.py:162
  17.3 1.3 collective-permute-start.1
  18.9 3.5 %all-to-all-done = s32[32,1,256]{2,1,0:T(1,128)S(1)} async-done(((s32[32,1,256]{2,1,0:T(1,128)}), s32[32,1,256]{2,1,0:T(1,128)S(1)}, u32[]{:S(2)}, u32[]{:S(2)}) %all-to-all-start) | async-done | bytes 32800 | tf_op jit(solution)/shard_map/all_to_all | solution.py:170
  22.5 7.3 %fusion.8 = bf16[2048,512]{1,0:T(8,128)(2,1)} fusion(s32[2048]{0:T(1024)S(1)} %bitcast.77, bf16[2,2048,512]{2,1,0:T(8,128)(2,1)} %param.14), kind=kOutput, calls=%fused_computation.24 | convolution fusion | flops 4300210176 | bytes 4202496 | tf_op jit(solution)/shard_map/dot_general | solution.py:127
  29.8 4.8 %all-to-all-start.1 = ((bf16[16,128,512]{2,1,0:T(8,128)(2,1)}), bf16[16,128,512]{2,1,0:T(8,128)(2,1)}, u32[]{:S(2)}, u32[]{:S(2)}) async-start(bf16[16,128,512]{2,1,0:T(8,128)(2,1)} %bitcast.23), calls=%async_computation.1 | async-start | bytes 4194304 | tf_op jit(solution)/shard_map/all_to_all | solution.py:174
  35.8 13.8 %fusion.19 = bf16[4,2,128,512]{3,0,2,1:T(4,128)(2,1)S(1)} fusion(bf16[3,3,512,512]{3,2,1,0:T(8,128)(2,1)} %param.12, bf16[4,4,128,512]{3,2,1,0:T(8,128)(2,1)S(1)} %bitcast.60), kind=kOutput, calls=%fused_computation.36 | convolution fusion | flops 4809293824 | bytes 7864320 | tf_op jit(solution)/shard_map/conv_general_dilated | solution.py:17
  49.8 3.4 %collective-permute-start.2 = (bf16[2,2,2,128,512]{4,3,2,1,0:T(8,128)(2,1)S(1)}, bf16[2,2,2,128,512]{4,3,2,1,0:T(8,128)(2,1)S(1)}, u32[]{:S(2)}, u32[]{:S(2)}) collective-permute-start(bf16[2,2,2,128,512]{4,3,2,1,0:T(8,128)(2,1)S(1)} %bitcast.55), channel_id=1, source_target_pairs={{0,16},{1,17},{2,18},{3,19},{4,20},{5,21},{6,22},{7,23},{8,24},{9,... | collective-permute-start | bytes 3145736 | tf_op jit(solution)/shard_map/ppermute | solution.py:180
  53.3 1.5 slice.45
  54.7 8.0 %fusion.5 = bf16[4096,256]{1,0:T(8,128)(2,1)} fusion(s32[4096]{0:T(1024)S(1)} %bitcast.69, bf16[1,2048,512]{2,1,0:T(8,128)(2,1)} %slice.45, s32[]{:T(128)S(6)} %select_n.22), kind=kOutput, calls=%fused_computation.16 | convolution fusion | flops 4304404480 | bytes 3162116 | tf_op jit(solution)/shard_map/dot_general | solution.py:127
  62.8 13.3 %collective-permute-done.2 = bf16[2,2,2,128,512]{4,3,2,1,0:T(8,128)(2,1)S(1)} collective-permute-done((bf16[2,2,2,128,512]{4,3,2,1,0:T(8,128)(2,1)S(1)}, bf16[2,2,2,128,512]{4,3,2,1,0:T(8,128)(2,1)S(1)}, u32[]{:S(2)}, u32[]{:S(2)}) %collective-permute-start.2) | collective-permute-done | bytes 1048608 | tf_op jit(solution)/shard_map/ppermute | solution.py:180
  76.1 1.6 fusion.12
  77.7 5.0 %pack.3 = bf16[2,2048,256]{2,1,0:T(8,128)(2,1)} custom-call(s32[1,1024]{1,0:T(1,128)} %get-tuple-element.19.slot_ref, bf16[1024,512]{1,0:T(8,128)(2,1)} %bitcast.61), custom_call_target="tpu_custom_call" | custom-call | flops 2147483648 | bytes 6291456 | tf_op jit(solution)/shard_map/pack/pallas_call | solution.py:66
  82.8 6.6 %all-to-all-start.3 = ((bf16[32,128,256]{2,1,0:T(8,128)(2,1)}), bf16[32,128,256]{2,1,0:T(8,128)(2,1)S(1)}, u32[]{:S(2)}, u32[]{:S(2)}) async-start(bf16[32,128,256]{2,1,0:T(8,128)(2,1)} %bitcast.59), calls=%async_computation.3 | async-start | bytes 4194304 | tf_op jit(solution)/shard_map/all_to_all | solution.py:204
  89.4 5.0 %subtract_convert_fusion.vector_ref = bf16[1024,512]{1,0:T(8,128)(2,1)} fusion(bf16[1024,512]{1,0:T(8,128)(2,1)S(1)} %bitcast.62, bf16[2048,512]{1,0:T(8,128)(2,1)} %bitcast.24, s32[1024]{0:T(1024)S(1)} %bitcast.82), kind=kOutput, calls=%fused_computation.34 | convolution fusion | flops 2152202240 | bytes 4198400 | tf_op jit(solution)/shard_map/dot_general | solution.py:127
  94.4 5.0 %pack.2 = bf16[2,2048,256]{2,1,0:T(8,128)(2,1)} custom-call(s32[1,1024]{1,0:T(1,128)} %get-tuple-element.20.slot_ref, bf16[1024,512]{1,0:T(8,128)(2,1)} %subtract_convert_fusion.vector_ref), custom_call_target="tpu_custom_call" | custom-call | flops 2147483648 | bytes 6291456 | tf_op jit(solution)/shard_map/pack/pallas_call | solution.py:66
  99.4 39.7 %all-to-all-done.3 = bf16[32,128,256]{2,1,0:T(8,128)(2,1)S(1)} async-done(((bf16[32,128,256]{2,1,0:T(8,128)(2,1)}), bf16[32,128,256]{2,1,0:T(8,128)(2,1)S(1)}, u32[]{:S(2)}, u32[]{:S(2)}) %all-to-all-start.3) | async-done | bytes 2097184 | tf_op jit(solution)/shard_map/all_to_all | solution.py:204
  139.1 1.3 copy-done.2
  140.4 2.9 %all-to-all-start.2 = ((bf16[32,128,256]{2,1,0:T(8,128)(2,1)}), bf16[32,128,256]{2,1,0:T(8,128)(2,1)S(1)}, u32[]{:S(2)}, u32[]{:S(2)}) async-start(bf16[32,128,256]{2,1,0:T(8,128)(2,1)} %bitcast.58), calls=%async_computation.2 | async-start | bytes 4194304 | tf_op jit(solution)/shard_map/all_to_all | solution.py:204
  143.4 3.4 %convert_reduce_fusion = f32[2048]{0:T(1024)S(1)} fusion(s32[4096]{0:T(1024)S(1)} %bitcast.70), kind=kLoop, calls=%fused_computation.1 | loop fusion | flops 25163776 | bytes 24576 | tf_op jit(solution)/shard_map/reduce_sum | solution.py:187
  146.8 3.4 %convert_reduce_fusion.1 = f32[2048]{0:T(1024)S(1)} fusion(s32[4096]{0:T(1024)S(1)} %bitcast.66), kind=kLoop, calls=%fused_computation.3 | loop fusion | flops 25163776 | bytes 24576 | tf_op jit(solution)/shard_map/reduce_sum | solution.py:187
  150.2 0.7 fusion.31
  150.9 9.3 %tally.2.rest_0_ = f32[2,2048,256]{2,1,0:T(8,128)} custom-call(f32[2]{0:T(128)} %decay_ref.3, s32[1,4096]{1,0:T(1,128)} %bitcast.67, bf16[4096,256]{1,0:T(8,128)(2,1)} %bitcast.57, f32[2,2048,256]{2,1,0:T(8,128)} %old_ref.3), custom_call_target="tpu_custom_call" | custom-call | flops 4294967296 | bytes 4194304 | tf_op jit(solution)/shard_map/tally/pallas_call | solution.py:108
  160.1 32.7 %all-to-all-done.2 = bf16[32,128,256]{2,1,0:T(8,128)(2,1)S(1)} async-done(((bf16[32,128,256]{2,1,0:T(8,128)(2,1)}), bf16[32,128,256]{2,1,0:T(8,128)(2,1)S(1)}, u32[]{:S(2)}, u32[]{:S(2)}) %all-to-all-start.2) | async-done | bytes 2097184 | tf_op jit(solution)/shard_map/all_to_all | solution.py:204
  192.8 3.7 %multiply_reduce_fusion = f32[4096]{0:T(1024)} fusion(bf16[4096,256]{1,0:T(8,128)(2,1)} %fusion.5, bf16[32,128,256]{2,1,0:T(8,128)(2,1)S(1)} %all-to-all-done.2), kind=kLoop, calls=%fused_computation.17 | loop fusion | flops 5238784 | bytes 4210688 | tf_op jit(solution)/shard_map/reduce_sum | solution.py:213
  196.5 2.5 %all-to-all-start.4 = ((f32[32,1,128]{2,1,0:T(1,128)}), f32[32,1,128]{2,1,0:T(1,128)S(1)}, u32[]{:S(2)}, u32[]{:S(2)}) async-start(f32[32,1,128]{2,1,0:T(1,128)} %bitcast.31), calls=%async_computation.4 | async-start | bytes 32768 | tf_op jit(solution)/shard_map/all_to_all | solution.py:214
  199.1 9.3 %tally.3 = f32[2,2048,256]{2,1,0:T(8,128)} custom-call(f32[2]{0:T(128)} %decay_ref.3, s32[1,4096]{1,0:T(1,128)} %bitcast.71, bf16[4096,256]{1,0:T(8,128)(2,1)} %bitcast.54, f32[2,2048,256]{2,1,0:T(8,128)} %old_ref.3, f32[2,2048,256]{2,1,0:T(8,128)} %tally.2.rest_0_), custom_call_target="tpu_custom_call", output_to_operand_aliasing={{}: (4, {})} | custom-call | flops 4294967296 | bytes 4194304 | tf_op jit(solution)/shard_map/tally/pallas_call | solution.py:108
  209.6 1.2 select_reduce_fusion.1
  (54 shorter events, 4.8 us)
Async XLA Ops:
  0.6 18.0 %copy-start = (bf16[2,2,2,128,512]{4,3,2,1,0:T(8,128)(2,1)S(1)}, bf16[2,2,2,128,512]{4,3,2,1,0:T(8,128)(2,1)}, u32[]{:S(2)}) copy-start(bf16[2,2,2,128,512]{4,3,2,1,0:T(8,128)(2,1)} %param.10) | copy-start | bytes 3145732
  7.8 14.6 %all-to-all-start = ((s32[32,1,256]{2,1,0:T(1,128)}), s32[32,1,256]{2,1,0:T(1,128)S(1)}, u32[]{:S(2)}, u32[]{:S(2)}) async-start(s32[32,1,256]{2,1,0:T(1,128)} %bitcast.7), calls=%async_computation | async-start | bytes 65536 | tf_op jit(solution)/shard_map/all_to_all | solution.py:170
  15.1 20.4 %collective-permute-start = (bf16[2,2,1,128,512]{4,3,2,1,0:T(8,128)(2,1)S(1)}, bf16[2,2,1,128,512]{4,3,2,1,0:T(8,128)(2,1)S(1)}, u32[]{:S(2)}, u32[]{:S(2)}) collective-permute-start(bf16[2,2,1,128,512]{4,3,2,1,0:T(8,128)(2,1)S(1)} %get-tuple-element.9), channel_id=1, source_target_pairs={{0,1},{1,2},{2,3},{3,4},{4,5},{5,6},{6,7},{7,8},{8,9},{9,10},{10,1... | collective-permute-start | bytes 1572872 | tf_op jit(solution)/shard_map/ppermute | solution.py:162
  17.3 18.2 %collective-permute-start.1 = (bf16[2,2,1,128,512]{4,3,2,1,0:T(8,128)(2,1)S(1)}, bf16[2,2,1,128,512]{4,3,2,1,0:T(8,128)(2,1)S(1)}, u32[]{:S(2)}, u32[]{:S(2)}) collective-permute-start(bf16[2,2,1,128,512]{4,3,2,1,0:T(8,128)(2,1)S(1)} %get-tuple-element.10), channel_id=1, source_target_pairs={{1,0},{2,1},{3,2},{4,3},{5,4},{6,5},{7,6},{8,7},{9,8},{10,9},{11,1... | collective-permute-start | bytes 1572872 | tf_op jit(solution)/shard_map/ppermute | solution.py:163
  22.4 121.0 %copy-start.7 = (s32[2,16,1,128]{3,2,1,0:T(1,128)}, s32[2,16,1,128]{3,2,1,0:T(1,128)S(1)}, u32[]{:S(2)}) copy-start(s32[2,16,1,128]{3,2,1,0:T(1,128)S(1)} %get-tuple-element.18) | copy-start | bytes 49156
  22.4 124.3 %copy-start.5 = (s32[2,16,1,128]{3,2,1,0:T(1,128)}, s32[2,16,1,128]{3,2,1,0:T(1,128)S(1)}, u32[]{:S(2)}) copy-start(s32[2,16,1,128]{3,2,1,0:T(1,128)S(1)} %get-tuple-element.17) | copy-start | bytes 49156
  29.8 5.4 %copy-start.8 = (f32[512]{0:T(512)S(1)}, f32[512]{0:T(512)}, u32[]{:S(2)}) copy-start(f32[512]{0:T(512)} %param.11) | copy-start | bytes 6148
  29.8 52.9 %all-to-all-start.1 = ((bf16[16,128,512]{2,1,0:T(8,128)(2,1)}), bf16[16,128,512]{2,1,0:T(8,128)(2,1)}, u32[]{:S(2)}, u32[]{:S(2)}) async-start(bf16[16,128,512]{2,1,0:T(8,128)(2,1)} %bitcast.23), calls=%async_computation.1 | async-start | bytes 4194304 | tf_op jit(solution)/shard_map/all_to_all | solution.py:174
  35.8 17.5 %copy-start.4 = (bf16[2,2048,512]{2,1,0:T(8,128)(2,1)S(1)}, bf16[2,2048,512]{2,1,0:T(8,128)(2,1)}, u32[]{:S(2)}) copy-start(bf16[2,2048,512]{2,1,0:T(8,128)(2,1)} %param.14) | copy-start | bytes 12582916
  49.6 3.6 %copy-start.9 = (f32[3,512]{1,0:T(4,128)S(1)}, f32[3,512]{1,0:T(4,128)}, u32[]{:S(2)}) copy-start(f32[3,512]{1,0:T(4,128)} %param.13) | copy-start | bytes 18436
  49.8 26.3 %collective-permute-start.2 = (bf16[2,2,2,128,512]{4,3,2,1,0:T(8,128)(2,1)S(1)}, bf16[2,2,2,128,512]{4,3,2,1,0:T(8,128)(2,1)S(1)}, u32[]{:S(2)}, u32[]{:S(2)}) collective-permute-start(bf16[2,2,2,128,512]{4,3,2,1,0:T(8,128)(2,1)S(1)} %bitcast.55), channel_id=1, source_target_pairs={{0,16},{1,17},{2,18},{3,19},{4,20},{5,21},{6,22},{7,23},{8,24},{9,... | collective-permute-start | bytes 3145736 | tf_op jit(solution)/shard_map/ppermute | solution.py:180
  82.7 6.6 %copy-start.3 = (bf16[2,2,2,128,512]{4,3,2,1,0:T(8,128)(2,1)S(1)}, bf16[2,2,2,128,512]{4,3,2,1,0:T(8,128)(2,1)}, u32[]{:S(2)}) copy-start(bf16[2,2,2,128,512]{4,3,2,1,0:T(8,128)(2,1)} %fusion.12) | copy-start | bytes 3145732
  82.8 6.6 %copy-start.11 = (s32[1,1024]{1,0:T(1,128)S(1)}, s32[1,1024]{1,0:T(1,128)}, u32[]{:S(2)}) copy-start(s32[1,1024]{1,0:T(1,128)} %get-tuple-element.19.slot_ref) | copy-start | bytes 12292
  82.8 56.3 %all-to-all-start.3 = ((bf16[32,128,256]{2,1,0:T(8,128)(2,1)}), bf16[32,128,256]{2,1,0:T(8,128)(2,1)S(1)}, u32[]{:S(2)}, u32[]{:S(2)}) async-start(bf16[32,128,256]{2,1,0:T(8,128)(2,1)} %bitcast.59), calls=%async_computation.3 | async-start | bytes 4194304 | tf_op jit(solution)/shard_map/all_to_all | solution.py:204
  139.1 1.3 copy-start.2
  139.1 4.3 %copy-start.12 = (f32[2]{0:T(128)S(1)}, f32[2]{0:T(128)}, u32[]{:S(2)}) copy-start(f32[2]{0:T(128)} %decay_ref.3) | copy-start | bytes 28
  139.1 11.1 %copy-start.6 = (f32[2,2048]{1,0:T(2,128)S(1)}, f32[2,2048]{1,0:T(2,128)}, u32[]{:S(2)}) copy-start(f32[2,2048]{1,0:T(2,128)} %param.15) | copy-start | bytes 49156
  140.4 52.4 %all-to-all-start.2 = ((bf16[32,128,256]{2,1,0:T(8,128)(2,1)}), bf16[32,128,256]{2,1,0:T(8,128)(2,1)S(1)}, u32[]{:S(2)}, u32[]{:S(2)}) async-start(bf16[32,128,256]{2,1,0:T(8,128)(2,1)} %bitcast.58), calls=%async_computation.2 | async-start | bytes 4194304 | tf_op jit(solution)/shard_map/all_to_all | solution.py:204
  192.8 3.7 %copy-start.1 = (bf16[32,128,256]{2,1,0:T(8,128)(2,1)}, bf16[32,128,256]{2,1,0:T(8,128)(2,1)S(1)}, u32[]{:S(2)}) copy-start(bf16[32,128,256]{2,1,0:T(8,128)(2,1)S(1)} %all-to-all-done.2) | copy-start | bytes 6291460
  196.5 11.8 %all-to-all-start.4 = ((f32[32,1,128]{2,1,0:T(1,128)}), f32[32,1,128]{2,1,0:T(1,128)S(1)}, u32[]{:S(2)}, u32[]{:S(2)}) async-start(f32[32,1,128]{2,1,0:T(1,128)} %bitcast.31), calls=%async_computation.4 | async-start | bytes 32768 | tf_op jit(solution)/shard_map/all_to_all | solution.py:214
  199.1 10.6 %copy-start.10 = (s32[1,1024]{1,0:T(1,128)S(1)}, s32[1,1024]{1,0:T(1,128)}, u32[]{:S(2)}) copy-start(s32[1,1024]{1,0:T(1,128)} %get-tuple-element.20.slot_ref) | copy-start | bytes 12292
where the time goes:
time: 213 us; the launch traced here: 211 us
  waiting for transfers between devices  89.2 us (42%)
  matrix products  34.6 us (16%)
  starting transfers between devices  31.1 us (15%)
  Pallas kernels  28.6 us (13%)
  other arithmetic  22.1 us (10%)
  local copies, waits for them, and re-layouts  4.84 us (2%)
    all_to_all x2, waiting for transfers between devices, deliver(): lax.all_to_all(packed, everyone, split_axis=0, concat_axis=0, tiled=True)  72.4 us
    dot_general x3, matrix products, picked(): jnp.dot(rows_by(ids, table.shape[0]), table, preferred_element_type=jnp.f...  20.3 us
    pallas_call x2, Pallas kernels, tally(): pl.pallas_call(kernel, grid=(code_rows // block,), out_shape=jax.ShapeDty...  18.6 us
    conv_general_dilated x1, matrix products, convolve(): lax.conv_general_dilated(padded.reshape(clips * frames, rows, width, chan...  13.8 us
    ppermute x1, waiting for transfers between devices, body(): earlier = lax.ppermute(hidden, 'tm', [(i, i + 1) for i in range(slabs - 1)])  13.3 us
    pallas_call x2, Pallas kernels, pack(): pl.pallas_call(kernel, grid=(total // block,), out_shape=jax.ShapeDtypeSt...  10 us
    all_to_all x2, starting transfers between devices, deliver(): lax.all_to_all(packed, everyone, split_axis=0, concat_axis=0, tiled=True)  9.57 us
    all_to_all x1, starting transfers between devices, body(): lax.all_to_all(wanted, everyone, split_axis=0, concat_axis=0, tiled=True)  7.32 us
  transfers between devices with their start and end apart: 8, of which 4 were waited for; matrix products, arithmetic and copies ran while one was open for 22% of the time, Pallas kernels for 14%

commit v1 on v0

--- a/solution.py
+++ b/solution.py
@@ -79,44 +79,141 @@
     )(slot_ids[None, :], vectors)
 
 
-def tally(which, ids, vectors, ema_sums, decay, into):
-    amount, part = vectors.shape
+def exchange(first, second, first_ids, second_ids, second_quant, ema_sums, decay, slabs, num_peers):
+    members, capacity, part = first.shape
     code_rows = ema_sums.shape[1]
-    block = block_of(code_rows, 256)
-
-    def kernel(decay_ref, id_ref, vector_ref, old_ref, *rest):
-        out_ref = rest[-1]
-        start = pl.program_id(0) * block
-        places = start + lax.broadcasted_iota(jnp.int32, (block, amount), 0)
-        hot = jnp.where(places == id_ref[...], 1.0, 0.0).astype(jnp.bfloat16)
-        sums = jnp.dot(hot, vector_ref[...], preferred_element_type=jnp.float32)
-        keep = decay_ref[which]
-        out_ref[0] = keep * old_ref[0] + (1.0 - keep) * sums
-
-    operands = [decay, ids[None, :], vectors, ema_sums]
-    in_specs = [
-        pl.BlockSpec(memory_space=pltpu.SMEM),
-        pl.BlockSpec((1, amount), lambda i: (0, 0)),
-        pl.BlockSpec((amount, part), lambda i: (0, 0)),
-        pl.BlockSpec((1, block, part), lambda i: (which, i, 0)),
-    ]
-    aliases = {}
-    if into is not None:
-        operands.append(into)
-        in_specs.append(pl.BlockSpec(memory_space=pl.ANY))
-        aliases = {4: 0}
+    amount = members * capacity
+    block = code_rows
+    while block * amount > 2**20 and block % 2 == 0:
+        block //= 2
+    blocks = code_rows // block
+
+    def kernel(
+        first_ref,
+        second_ref,
+        first_id_ref,
+        second_id_ref,
+        quant_ref,
+        old_ref,
+        decay_ref,
+        sums_ref,
+        error_ref,
+        first_in,
+        second_in,
+        squares,
+        local_sems,
+        send_sems,
+        recv_sems,
+    ):
+        me_slab = lax.axis_index("tm")
+        me_row = lax.axis_index("height")
+        me = me_slab * num_peers + me_row
+
+        def peer_of(step):
+            peer = lax.rem(me + step, members)
+            return peer, {"tm": peer // num_peers, "height": lax.rem(peer, num_peers)}
+
+        barrier = pltpu.get_barrier_semaphore()
+
+        @pl.loop(1, members)
+        def _(step):
+            _, target = peer_of(step)
+            pl.semaphore_signal(
+                barrier, inc=1, device_id=target, device_id_type=pl.DeviceIdType.MESH
+            )
+
+        pl.semaphore_wait(barrier, members - 1)
+
+        def send(source, landing, which):
+            @pl.loop(1, members)
+            def _(step):
+                peer, target = peer_of(step)
+                pltpu.make_async_remote_copy(
+                    src_ref=source.at[peer],
+                    dst_ref=landing.at[me],
+                    send_sem=send_sems.at[which],
+                    recv_sem=recv_sems.at[which],
+                    device_id=target,
+                    device_id_type=pl.DeviceIdType.MESH,
+                ).start()
+
+        def own(source, landing, which):
+            return pltpu.make_async_copy(source.at[me], landing.at[me], local_sems.at[which])
+
+        def finish(landing, sems, which):
+            most = landing.at[pl.ds(0, members - 1)]
+            pltpu.make_async_copy(most, most, sems.at[which]).wait()
+
+        send(first_ref, first_in, 0)
+        send(second_ref, second_in, 1)
+        own(first_ref, first_in, 0).start()
+        own(second_ref, second_in, 1).start()
+
+        def tally(which, id_ref, landing, begin, end):
+            ids = id_ref[...]
+            keep = decay_ref[which]
+
+            @pl.loop(begin, end)
+            def _(step):
+                start = pl.multiple_of(step * block, block)
+                places = start + lax.broadcasted_iota(jnp.int32, (block, amount), 0)
+                hot = jnp.where(places == ids, 1.0, 0.0).astype(jnp.bfloat16)
+                vectors = landing[...].reshape(amount, part)
+                sums = jnp.dot(hot, vectors, preferred_element_type=jnp.float32)
+                here = pl.ds(start, block)
+                sums_ref[which, here, :] = keep * old_ref[which, here, :] + (1.0 - keep) * sums
+
+        own(first_ref, first_in, 0).wait()
+        finish(first_in, recv_sems, 0)
+        tally(0, first_id_ref, first_in, 0, blocks)
+        own(second_ref, second_in, 1).wait()
+        finish(second_in, recv_sems, 1)
+
+        @pl.loop(0, members)
+        def _(source):
+            leftover = second_in[source].astype(jnp.float32) - quant_ref[source].astype(jnp.float32)
+            squares[source] = jnp.sum(leftover * leftover, axis=1)[None, :]
+
+        tally(1, second_id_ref, second_in, 0, 1)
+        send(squares, error_ref, 2)
+        own(squares, error_ref, 2).start()
+        tally(1, second_id_ref, second_in, 1, blocks)
+        own(squares, error_ref, 2).wait()
+        finish(error_ref, recv_sems, 2)
+        finish(first_in, send_sems, 0)
+        finish(second_in, send_sems, 1)
+        finish(error_ref, send_sems, 2)
+
+    vmem = pl.BlockSpec(memory_space=pltpu.VMEM)
     return pl.pallas_call(
         kernel,
-        grid=(code_rows // block,),
-        out_shape=jax.ShapeDtypeStruct(ema_sums.shape, jnp.float32),
-        in_specs=in_specs,
-        out_specs=pl.BlockSpec((1, block, part), lambda i: (which, i, 0)),
-        input_output_aliases=aliases,
-        cost_estimate=pl.CostEstimate(
-            flops=2 * code_rows * amount * part, bytes_accessed=8 * code_rows * part, transcendentals=0
+        out_shape=(
+            jax.ShapeDtypeStruct(ema_sums.shape, jnp.float32),
+            jax.ShapeDtypeStruct((members, 1, capacity), jnp.float32),
         ),
-        name="tally",
-    )(*operands)
+        in_specs=[vmem] * 6 + [pl.BlockSpec(memory_space=pltpu.SMEM)],
+        out_specs=(vmem, vmem),
+        scratch_shapes=[
+            pltpu.VMEM(first.shape, jnp.bfloat16),
+            pltpu.VMEM(second.shape, jnp.bfloat16),
+            pltpu.VMEM((members, 1, capacity), jnp.float32),
+            pltpu.SemaphoreType.DMA((3,)),
+            pltpu.SemaphoreType.DMA((3,)),
+            pltpu.SemaphoreType.DMA((3,)),
+        ],
+        compiler_params=pltpu.CompilerParams(
+            collective_id=0, has_side_effects=True, vmem_limit_bytes=60 * 2**20
+        ),
+        name="exchange",
+    )(
+        first,
+        second,
+        first_ids[None, :],
+        second_ids[None, :],
+        second_quant.reshape(members, capacity, part),
+        ema_sums,
+        decay,
+    )
 
 
 def rows_by(ids, count):
@@ -199,26 +296,27 @@
     encoded = (widened + mixed).astype(jnp.bfloat16)
     flat = encoded.reshape(-1, channels)
 
-    def deliver(vectors, slot):
-        packed = pack(slot, vectors, total, slabs).reshape(slabs * num_peers, capacity, part)
-        there = lax.all_to_all(packed, everyone, split_axis=0, concat_axis=0, tiled=True)
-        return there.reshape(-1, part)
-
-    first_there = deliver(flat, slots[0])
+    def packed(vectors, slot):
+        return pack(slot, vectors, total, slabs).reshape(slabs * num_peers, capacity, part)
+
     first_quant = picked(slots[0], answer.reshape(total, channels))
     residual = (flat.astype(jnp.float32) - first_quant.astype(jnp.float32)).astype(jnp.bfloat16)
-    second_there = deliver(residual, slots[1])
-
-    leftover = second_there.astype(jnp.float32) - second_quant.astype(jnp.float32)
-    squares = jnp.sum(leftover * leftover, axis=-1).reshape(slabs * num_peers, capacity)
-    squares = lax.all_to_all(squares, everyone, split_axis=0, concat_axis=0, tiled=True)
+    ema_sums_new, squares = exchange(
+        packed(flat, slots[0]),
+        packed(residual, slots[1]),
+        first_ids,
+        second_ids,
+        second_quant,
+        ema_sums,
+        decay,
+        slabs,
+        num_peers,
+    )
     squares = jnp.sum(squares.reshape(slabs, total), axis=0)
     match = slots[1][:, None] == jnp.arange(total, dtype=jnp.int32)[None, :]
     error = jnp.sum(jnp.where(match, squares[None, :], 0.0), axis=1) / channels
     error = error.reshape(codes_first.shape)
 
-    ema_sums_new = tally(0, first_ids, first_there, ema_sums, decay, None)
-    ema_sums_new = tally(1, second_ids, second_there, ema_sums, decay, ema_sums_new)
     keep = decay[:, None]
     ema_counts_new = keep * ema_counts + (1.0 - keep) * counts
     return (ema_counts_new, ema_sums_new, error)

time: 213 us -> 227 us (1.066)
  Pallas kernels: 28.6 us -> 127 us
  waiting for transfers between devices: 89.2 us -> 17 us
  starting transfers between devices: 31.1 us -> 20.8 us
    pallas_call x2 -> x1, Pallas kernels: 18.6 us -> 117 us  [exchange(): pl.pallas_call(kernel, out_shape=(jax.ShapeDtypeStruct(ema_sums.shape, jn...]
    all_to_all x3 -> x0, waiting for transfers between devices: 72.4 us -> none  [the longest x2 72.4 us: deliver(): lax.all_to_all(packed, everyone, split_axis=0, concat_axis=0, tiled=True)]
    all_to_all x3 -> x0, starting transfers between devices: 12.1 us -> none  [the longest x2 9.57 us: deliver(): lax.all_to_all(packed, everyone, split_axis=0, concat_axis=0, tiled=True)]
    reduce_sum x1 -> x0, other arithmetic: 3.71 us -> none  [body(): jnp.sum(leftover * leftover, axis=-1).reshape(slabs * num_peers, capacity)]
    unnamed x27 -> x22, local copies, waits for them, and re-layouts: 1.38 us -> 4.52 us
  transfers between devices with their start and end apart: 8 -> 5, of which waited for: 4 -> 2; matrix products, arithmetic and copies ran while one was open for 22% -> 18% of each run, Pallas kernels for 14% -> 2%
where the time goes in v1:
time: 227 us
  Pallas kernels  127 us (56%)
  matrix products  33.6 us (15%)
  starting transfers between devices  20.8 us (9%)
  other arithmetic  20.3 us (9%)
  waiting for transfers between devices  17 us (7%)
  local copies, waits for them, and re-layouts  6.54 us (3%)
    pallas_call x1, Pallas kernels, exchange(): pl.pallas_call(kernel, out_shape=(jax.ShapeDtypeStruct(ema_sums.shape, jn...  117 us
    dot_general x3, matrix products, picked(): jnp.dot(rows_by(ids, table.shape[0]), table, preferred_element_type=jnp.f...  19.2 us
    ppermute x1, waiting for transfers between devices, body(): earlier = lax.ppermute(hidden, 'tm', [(i, i + 1) for i in range(slabs - 1)])  15.3 us
    conv_general_dilated x1, matrix products, convolve(): lax.conv_general_dilated(padded.reshape(clips * frames, rows, width, chan...  13.8 us
    pallas_call x2, Pallas kernels, pack(): pl.pallas_call(kernel, grid=(total // block,), out_shape=jax.ShapeDtypeSt...  10.1 us
    all_to_all x1, starting transfers between devices, body(): lax.all_to_all(wanted, everyone, split_axis=0, concat_axis=0, tiled=True)  7.32 us
    reduce_sum x2, other arithmetic, body(): jnp.sum((marks == ids[None, :]).astype(jnp.float32), axis=1)  6.77 us
    all_to_all x1, starting transfers between devices, body(): lax.all_to_all(answer, 'height', split_axis=0, concat_axis=0, tiled=True)  5.61 us
  transfers between devices with their start and end apart: 5, of which 2 were waited for; matrix products, arithmetic and copies ran while one was open for 18% of the time, Pallas kernels for 2%

profile of v1, /device:TPU:0, one launch (start us, length us, event | category | flops | bytes accessed | tf_op | source)
XLA Modules:
  0.0 226.6 jit_solution(3678772154052762351)
XLA Ops:
  0.6 1.6 fusion.26
  2.2 0.7 pad_add_fusion
  3.0 1.5 fusion.28
  4.6 0.5 multiply_reduce_fusion
  5.1 2.0 select_reduce_fusion
  7.2 0.6 broadcast_in_dim.24
  7.8 7.3 %all-to-all-start = ((s32[32,1,256]{2,1,0:T(1,128)}), s32[32,1,256]{2,1,0:T(1,128)S(1)}, u32[]{:S(2)}, u32[]{:S(2)}) async-start(s32[32,1,256]{2,1,0:T(1,128)} %bitcast.7), calls=%async_computation | async-start | bytes 65536 | tf_op jit(solution)/shard_map/all_to_all | solution.py:267
  15.2 3.0 %collective-permute-start = (bf16[2,2,1,128,512]{4,3,2,1,0:T(8,128)(2,1)S(1)}, bf16[2,2,1,128,512]{4,3,2,1,0:T(8,128)(2,1)}, u32[]{:S(2)}, u32[]{:S(2)}) collective-permute-start(bf16[2,2,1,128,512]{4,3,2,1,0:T(8,128)(2,1)S(1)} %get-tuple-element.11), channel_id=1, source_target_pairs={{0,1},{1,2},{2,3},{3,4},{4,5},{5,6},{6,7},{7,8},{8,9},{9,10},{10,1... | collective-permute-start | bytes 1572872 | tf_op jit(solution)/shard_map/ppermute | solution.py:259
  18.1 1.3 collective-permute-start.1
  19.7 0.6 fusion.34
  20.3 0.3 fusion.11
  20.7 1.7 all-to-all-done
  22.5 7.4 %fusion.8 = bf16[2048,512]{1,0:T(8,128)(2,1)} fusion(s32[2048]{0:T(1024)S(1)} %bitcast.74, bf16[2,2048,512]{2,1,0:T(8,128)(2,1)} %param.14), kind=kOutput, calls=%fused_computation.23 | convolution fusion | flops 4300210176 | bytes 4202496 | tf_op jit(solution)/shard_map/dot_general | solution.py:224
  29.8 5.6 %all-to-all-start.1 = ((bf16[16,128,512]{2,1,0:T(8,128)(2,1)}), bf16[16,128,512]{2,1,0:T(8,128)(2,1)}, u32[]{:S(2)}, u32[]{:S(2)}) async-start(bf16[16,128,512]{2,1,0:T(8,128)(2,1)} %bitcast.53), calls=%async_computation.1 | async-start | bytes 4194304 | tf_op jit(solution)/shard_map/all_to_all | solution.py:271
  35.5 3.4 %convert_reduce_fusion.1 = f32[2048]{0:T(1024)S(1)} fusion(s32[4096]{0:T(1024)S(1)} %bitcast.62), kind=kLoop, calls=%fused_computation.3 | loop fusion | flops 25163776 | bytes 24576 | tf_op jit(solution)/shard_map/reduce_sum | solution.py:284
  38.9 3.4 %convert_reduce_fusion = f32[2048]{0:T(1024)S(1)} fusion(s32[4096]{0:T(1024)S(1)} %bitcast.64), kind=kLoop, calls=%fused_computation.1 | loop fusion | flops 25163776 | bytes 24576 | tf_op jit(solution)/shard_map/reduce_sum | solution.py:284
  42.3 1.4 pad_maximum_fusion
  43.7 13.8 %fusion.19 = bf16[4,2,128,512]{3,0,2,1:T(4,128)(2,1)S(1)} fusion(bf16[3,3,512,512]{3,2,1,0:T(8,128)(2,1)} %param.12, bf16[4,4,128,512]{3,2,1,0:T(8,128)(2,1)S(1)} %bitcast.54), kind=kOutput, calls=%fused_computation.35 | convolution fusion | flops 4809293824 | bytes 7864320 | tf_op jit(solution)/shard_map/conv_general_dilated | solution.py:17
  57.8 3.6 %collective-permute-start.2 = (bf16[2,2,2,128,512]{4,3,2,1,0:T(8,128)(2,1)S(1)}, bf16[2,2,2,128,512]{4,3,2,1,0:T(8,128)(2,1)S(1)}, u32[]{:S(2)}, u32[]{:S(2)}) collective-permute-start(bf16[2,2,2,128,512]{4,3,2,1,0:T(8,128)(2,1)S(1)} %bitcast.51), channel_id=1, source_target_pairs={{0,16},{1,17},{2,18},{3,19},{4,20},{5,21},{6,22},{7,23},{8,24},{9,... | collective-permute-start | bytes 3145736 | tf_op jit(solution)/shard_map/ppermute | solution.py:277
  61.4 0.7 fusion.31
  62.1 6.9 %fusion.5 = bf16[4096,256]{1,0:T(8,128)(2,1)} fusion(s32[4096]{0:T(1024)S(1)} %bitcast.65, bf16[1,2048,512]{2,1,0:T(8,128)(2,1)S(1)} %slice-done, s32[]{:T(128)S(6)} %select_n.22), kind=kOutput, calls=%fused_computation.16 | convolution fusion | flops 4304404480 | bytes 3162116 | tf_op jit(solution)/shard_map/dot_general | solution.py:224
  69.0 15.3 %collective-permute-done.2 = bf16[2,2,2,128,512]{4,3,2,1,0:T(8,128)(2,1)S(1)} collective-permute-done((bf16[2,2,2,128,512]{4,3,2,1,0:T(8,128)(2,1)S(1)}, bf16[2,2,2,128,512]{4,3,2,1,0:T(8,128)(2,1)S(1)}, u32[]{:S(2)}, u32[]{:S(2)}) %collective-permute-start.2) | collective-permute-done | bytes 1048608 | tf_op jit(solution)/shard_map/ppermute | solution.py:277
  84.2 1.7 fusion.12
  85.9 5.1 %pack.2 = bf16[2,2048,256]{2,1,0:T(8,128)(2,1)} custom-call(s32[1,1024]{1,0:T(1,128)} %get-tuple-element.24.slot_ref, bf16[1024,512]{1,0:T(8,128)(2,1)} %bitcast.58), custom_call_target="tpu_custom_call" | custom-call | flops 2147483648 | bytes 6291456 | tf_op jit(solution)/shard_map/pack/pallas_call | solution.py:66
  91.0 5.0 %subtract_convert_fusion.vector_ref = bf16[1024,512]{1,0:T(8,128)(2,1)} fusion(bf16[1024,512]{1,0:T(8,128)(2,1)S(1)} %bitcast.59, bf16[2048,512]{1,0:T(8,128)(2,1)} %bitcast.24, s32[1024]{0:T(1024)S(1)} %bitcast.79), kind=kOutput, calls=%fused_computation.33 | convolution fusion | flops 2152202240 | bytes 4198400 | tf_op jit(solution)/shard_map/dot_general | solution.py:224
  95.9 5.0 %pack.3 = bf16[2,2048,256]{2,1,0:T(8,128)(2,1)} custom-call(s32[1,1024]{1,0:T(1,128)} %get-tuple-element.23.slot_ref, bf16[1024,512]{1,0:T(8,128)(2,1)} %subtract_convert_fusion.vector_ref), custom_call_target="tpu_custom_call" | custom-call | flops 2147483648 | bytes 6291456 | tf_op jit(solution)/shard_map/pack/pallas_call | solution.py:66
  101.0 117.3 %exchange.1 = (f32[2,2048,256]{2,1,0:T(8,128)}, f32[32,1,128]{2,1,0:T(1,128)}) custom-call(bf16[32,128,256]{2,1,0:T(8,128)(2,1)} %bitcast.56, bf16[32,128,256]{2,1,0:T(8,128)(2,1)} %bitcast.57, s32[1,4096]{1,0:T(1,128)} %bitcast.63, s32[1,4096]{1,0:T(1,128)} %bitcast.66, bf16[32,128,256]{2,1,0:T(8,128)(2,1)} %bitcast.55, f32[2,2048,256]{2,1,0:T(8,128)} %old_ref.1, ...), custom_call_target="tpu_custom_call" | custom-call | tf_op jit(solution)/shard_map/exchange/pallas_call | solution.py:188
  218.3 0.5 broadcast.96
  218.8 1.4 reduce.5
  220.3 1.2 select_reduce_fusion.1
  221.5 0.6 broadcast_multiply_fusion
  222.1 4.5 %copy.43 = f32[2,2048,256]{2,1,0:T(8,128)} copy(f32[2,2048,256]{2,1,0:T(8,128)} %get-tuple-element.36) | data formatting | bytes 8388608
  (42 shorter events, 0.7 us)
Async XLA Ops:
  0.6 18.8 %copy-start = (bf16[2,2,2,128,512]{4,3,2,1,0:T(8,128)(2,1)S(1)}, bf16[2,2,2,128,512]{4,3,2,1,0:T(8,128)(2,1)}, u32[]{:S(2)}) copy-start(bf16[2,2,2,128,512]{4,3,2,1,0:T(8,128)(2,1)} %param.10) | copy-start | bytes 3145732
  2.2 18.1 %copy-start.5 = (f32[512]{0:T(512)S(1)}, f32[512]{0:T(512)}, u32[]{:S(2)}) copy-start(f32[512]{0:T(512)} %param.11) | copy-start | bytes 6148
  4.5 16.2 %copy-start.6 = (f32[3,512]{1,0:T(4,128)S(1)}, f32[3,512]{1,0:T(4,128)}, u32[]{:S(2)}) copy-start(f32[3,512]{1,0:T(4,128)} %param.13) | copy-start | bytes 18436
  4.5 16.2 %copy-start.9 = (f32[2]{0:T(128)S(1)}, f32[2]{0:T(128)}, u32[]{:S(2)}) copy-start(f32[2]{0:T(128)} %decay_ref.1) | copy-start | bytes 28
  7.8 14.6 %all-to-all-start = ((s32[32,1,256]{2,1,0:T(1,128)}), s32[32,1,256]{2,1,0:T(1,128)S(1)}, u32[]{:S(2)}, u32[]{:S(2)}) async-start(s32[32,1,256]{2,1,0:T(1,128)} %bitcast.7), calls=%async_computation | async-start | bytes 65536 | tf_op jit(solution)/shard_map/all_to_all | solution.py:267
  15.2 27.1 %collective-permute-start = (bf16[2,2,1,128,512]{4,3,2,1,0:T(8,128)(2,1)S(1)}, bf16[2,2,1,128,512]{4,3,2,1,0:T(8,128)(2,1)}, u32[]{:S(2)}, u32[]{:S(2)}) collective-permute-start(bf16[2,2,1,128,512]{4,3,2,1,0:T(8,128)(2,1)S(1)} %get-tuple-element.11), channel_id=1, source_target_pairs={{0,1},{1,2},{2,3},{3,4},{4,5},{5,6},{6,7},{7,8},{8,9},{9,10},{10,1... | collective-permute-start | bytes 1572872 | tf_op jit(solution)/shard_map/ppermute | solution.py:259
  18.1 24.1 %collective-permute-start.1 = (bf16[2,2,1,128,512]{4,3,2,1,0:T(8,128)(2,1)S(1)}, bf16[2,2,1,128,512]{4,3,2,1,0:T(8,128)(2,1)}, u32[]{:S(2)}, u32[]{:S(2)}) collective-permute-start(bf16[2,2,1,128,512]{4,3,2,1,0:T(8,128)(2,1)S(1)} %get-tuple-element.12), channel_id=1, source_target_pairs={{1,0},{2,1},{3,2},{4,3},{5,4},{6,5},{7,6},{8,7},{9,8},{10,9},{11,1... | collective-permute-start | bytes 1572872 | tf_op jit(solution)/shard_map/ppermute | solution.py:260
  22.5 13.0 %copy-start.2 = (s32[2,16,1,128]{3,2,1,0:T(1,128)}, s32[2,16,1,128]{3,2,1,0:T(1,128)S(1)}, u32[]{:S(2)}) copy-start(s32[2,16,1,128]{3,2,1,0:T(1,128)S(1)} %get-tuple-element.21) | copy-start | bytes 49156
  22.5 39.6 %copy-start.3 = (s32[2,16,1,128]{3,2,1,0:T(1,128)}, s32[2,16,1,128]{3,2,1,0:T(1,128)S(1)}, u32[]{:S(2)}) copy-start(s32[2,16,1,128]{3,2,1,0:T(1,128)S(1)} %get-tuple-element.22) | copy-start | bytes 49156
  29.8 61.1 %all-to-all-start.1 = ((bf16[16,128,512]{2,1,0:T(8,128)(2,1)}), bf16[16,128,512]{2,1,0:T(8,128)(2,1)}, u32[]{:S(2)}, u32[]{:S(2)}) async-start(bf16[16,128,512]{2,1,0:T(8,128)(2,1)} %bitcast.53), calls=%async_computation.1 | async-start | bytes 4194304 | tf_op jit(solution)/shard_map/all_to_all | solution.py:271
  43.7 17.7 %copy-start.4 = (f32[2,2048]{1,0:T(2,128)S(1)}, f32[2,2048]{1,0:T(2,128)}, u32[]{:S(2)}) copy-start(f32[2,2048]{1,0:T(2,128)} %param.15) | copy-start | bytes 49156
  57.6 4.5 %slice-start = ((bf16[2,2048,512]{2,1,0:T(8,128)(2,1)}), bf16[1,2048,512]{2,1,0:T(8,128)(2,1)S(1)}, s32[]{:S(2)}) async-start(bf16[2,2048,512]{2,1,0:T(8,128)(2,1)} %param.14), calls=%async_computation.2 | async-start | bytes 4194304 | tf_op jit(solution)/shard_map/slice | solution.py:279
  57.8 26.4 %collective-permute-start.2 = (bf16[2,2,2,128,512]{4,3,2,1,0:T(8,128)(2,1)S(1)}, bf16[2,2,2,128,512]{4,3,2,1,0:T(8,128)(2,1)S(1)}, u32[]{:S(2)}, u32[]{:S(2)}) collective-permute-start(bf16[2,2,2,128,512]{4,3,2,1,0:T(8,128)(2,1)S(1)} %bitcast.51), channel_id=1, source_target_pairs={{0,16},{1,17},{2,18},{3,19},{4,20},{5,21},{6,22},{7,23},{8,24},{9,... | collective-permute-start | bytes 3145736 | tf_op jit(solution)/shard_map/ppermute | solution.py:277
  85.9 5.1 %copy-start.1 = (bf16[2,2,2,128,512]{4,3,2,1,0:T(8,128)(2,1)S(1)}, bf16[2,2,2,128,512]{4,3,2,1,0:T(8,128)(2,1)}, u32[]{:S(2)}) copy-start(bf16[2,2,2,128,512]{4,3,2,1,0:T(8,128)(2,1)} %fusion.12) | copy-start | bytes 3145732
  85.9 5.1 %copy-start.8 = (s32[1,1024]{1,0:T(1,128)S(1)}, s32[1,1024]{1,0:T(1,128)}, u32[]{:S(2)}) copy-start(s32[1,1024]{1,0:T(1,128)} %get-tuple-element.24.slot_ref) | copy-start | bytes 12292
  101.0 119.3 %copy-start.7 = (s32[1,1024]{1,0:T(1,128)S(1)}, s32[1,1024]{1,0:T(1,128)}, u32[]{:S(2)}) copy-start(s32[1,1024]{1,0:T(1,128)} %get-tuple-element.23.slot_ref) | copy-start | bytes 12292

commit v2 on v1

--- a/solution.py
+++ b/solution.py
@@ -12,34 +12,155 @@
     return (widened * inverse * norm_gain).astype(jnp.bfloat16)
 
 
-def convolve(padded, kernel):
-    clips, frames, rows, width, channels = padded.shape
-    summed = lax.conv_general_dilated(
-        padded.reshape(clips * frames, rows, width, channels),
+def convolve(latents, norm_gain, row_before, row_after, kernel):
+    clips, frames, rows, width, channels = latents.shape
+    images = clips * frames
+
+    def body(latent_ref, gain_ref, before_ref, after_ref, weight_ref, out_ref):
+        normed = normalize(latent_ref[0].reshape(rows * width, channels), gain_ref[...])
+        taps = jnp.concatenate([before_ref[0], normed, after_ref[0]], axis=0)
+        windows = [taps[row * width : (row + rows) * width] for row in range(3)]
+        column = lax.broadcasted_iota(jnp.int32, (rows * width, channels), 0) % width
+
+        def tap(col):
+            total = jnp.dot(windows[0], weight_ref[0, col], preferred_element_type=jnp.float32)
+            for row in (1, 2):
+                total += jnp.dot(
+                    windows[row], weight_ref[row, col], preferred_element_type=jnp.float32
+                )
+            return total
+
+        summed = tap(1)
+        summed += jnp.where(column == 0, 0.0, pltpu.roll(tap(0), 1, 0))
+        summed += jnp.where(column == width - 1, 0.0, pltpu.roll(tap(2), rows * width - 1, 0))
+        hidden = jax.nn.silu(summed).astype(jnp.bfloat16)
+        out_ref[0] = hidden.reshape(rows, width, channels)
+
+    hidden = pl.pallas_call(
+        body,
+        grid=(images,),
+        out_shape=jax.ShapeDtypeStruct((images, rows, width, channels), jnp.bfloat16),
+        in_specs=[
+            pl.BlockSpec((1, rows, width, channels), lambda i: (i, 0, 0, 0)),
+            pl.BlockSpec((1, channels), lambda i: (0, 0)),
+            pl.BlockSpec((1, width, channels), lambda i: (i, 0, 0)),
+            pl.BlockSpec((1, width, channels), lambda i: (i, 0, 0)),
+            pl.BlockSpec(kernel.shape, lambda i: (0, 0, 0, 0)),
+        ],
+        out_specs=pl.BlockSpec((1, rows, width, channels), lambda i: (i, 0, 0, 0)),
+        compiler_params=pltpu.CompilerParams(vmem_limit_bytes=40 * 2**20),
+        cost_estimate=pl.CostEstimate(
+            flops=18 * images * rows * width * channels * channels,
+            bytes_accessed=2 * kernel.size + 4 * latents.size,
+            transcendentals=latents.size,
+        ),
+        name="convolve",
+    )(
+        latents.reshape(images, rows, width, channels),
+        norm_gain[None, :],
+        row_before.reshape(images, width, channels),
+        row_after.reshape(images, width, channels),
         kernel,
-        (1, 1),
-        ((0, 0), (1, 1)),
-        dimension_numbers=("NHWC", "HWIO", "NHWC"),
-        preferred_element_type=jnp.float32,
     )
-    hidden = jax.nn.silu(summed).astype(jnp.bfloat16)
-    return hidden.reshape(clips, frames, rows - 2, width, channels)
-
-
-def slots_of(indices, num_peers, capacity, code_rows):
-    amount = indices.shape[1]
-    owners = indices // code_rows
-    markers = (owners[:, :, None] == jnp.arange(num_peers, dtype=jnp.int32)).astype(jnp.bfloat16)
-    steps = jnp.arange(amount, dtype=jnp.int32)
-    earlier = (steps[:, None] > steps[None, :]).astype(jnp.bfloat16)
-    before = jnp.einsum("ij,sjp->isp", earlier, markers, preferred_element_type=jnp.float32)
-    ranking = jnp.sum(before.swapaxes(0, 1) * markers.astype(jnp.float32), axis=2)
-    return owners * capacity + ranking.astype(jnp.int32)
-
-
-def wanted_of(indices, slot_ids, total):
-    match = slot_ids[:, None, :] == jnp.arange(total, dtype=jnp.int32)[None, :, None]
-    return jnp.sum(jnp.where(match, indices[:, None, :] + 1, 0), axis=2) - 1
+    return hidden.reshape(latents.shape)
+
+
+def ask(codes, num_peers, slabs, capacity, code_rows):
+    amount = codes.shape[1]
+    members = slabs * num_peers
+    total = num_peers * capacity
+
+    def kernel(code_ref, slot_ref, ids_ref, outgoing, local_sem, send_sem, recv_sem):
+        me_row = lax.axis_index("height")
+        me = lax.axis_index("tm") * num_peers + me_row
+
+        def peer_of(step):
+            peer = lax.rem(me + step, members)
+            row = lax.rem(peer, num_peers)
+            return row, {"tm": peer // num_peers, "height": row}
+
+        barrier = pltpu.get_barrier_semaphore()
+
+        @pl.loop(1, members)
+        def _(step):
+            _, target = peer_of(step)
+            pl.semaphore_signal(
+                barrier, inc=1, device_id=target, device_id_type=pl.DeviceIdType.MESH
+            )
+
+        owners = lax.broadcasted_iota(jnp.int32, (num_peers, amount), 0)
+        later = lax.broadcasted_iota(jnp.int32, (amount, amount), 1)
+        sooner = lax.broadcasted_iota(jnp.int32, (amount, amount), 0)
+        order = jnp.where(sooner < later, 1.0, 0.0).astype(jnp.bfloat16)
+        for which in range(2):
+            code = code_ref[which : which + 1, :]
+            local = code - owners * code_rows
+            mark = jnp.where((local >= 0) & (local < code_rows), 1.0, 0.0)
+            before = jnp.dot(
+                mark.astype(jnp.bfloat16), order, preferred_element_type=jnp.float32
+            )
+            place = mark * (before + (owners * capacity).astype(jnp.float32))
+            slot = jnp.sum(place, axis=0, keepdims=True)
+            local = jnp.sum(jnp.where(mark > 0.0, local, 0), axis=0, keepdims=True)
+            slot_ref[which : which + 1, :] = slot.astype(jnp.int32)
+            high = (local // 256).astype(jnp.float32)
+            low = (local % 256).astype(jnp.float32)
+            kind = lax.broadcasted_iota(jnp.int32, (16, amount), 0)
+            digits = jnp.where(kind == 0, high, jnp.where(kind == 1, low, 1.0))
+            digits = digits.astype(jnp.bfloat16)
+            places = lax.broadcasted_iota(jnp.int32, (total, amount), 0).astype(jnp.float32)
+            hot = jnp.where(places == slot, 1.0, 0.0).astype(jnp.bfloat16)
+            found = lax.dot_general(
+                digits, hot, (((1,), (1,)), ((), ())), preferred_element_type=jnp.float32
+            )
+            wanted = found[0:1] * 256.0 + found[1:2] + found[2:3] - 1.0
+            wanted = wanted.astype(jnp.int32)
+            for row in range(num_peers):
+                outgoing[row, which : which + 1, :] = wanted[
+                    :, row * capacity : (row + 1) * capacity
+                ]
+
+        pl.semaphore_wait(barrier, members - 1)
+
+        @pl.loop(1, members)
+        def _(step):
+            row, target = peer_of(step)
+            pltpu.make_async_remote_copy(
+                src_ref=outgoing.at[row],
+                dst_ref=ids_ref.at[me],
+                send_sem=send_sem,
+                recv_sem=recv_sem,
+                device_id=target,
+                device_id_type=pl.DeviceIdType.MESH,
+            ).start()
+
+        own = pltpu.make_async_copy(outgoing.at[me_row], ids_ref.at[me], local_sem)
+        own.start()
+        own.wait()
+        most = ids_ref.at[pl.ds(0, members - 1)]
+        pltpu.make_async_copy(most, most, recv_sem).wait()
+        pltpu.make_async_copy(most, most, send_sem).wait()
+
+    vmem = pl.BlockSpec(memory_space=pltpu.VMEM)
+    return pl.pallas_call(
+        kernel,
+        out_shape=(
+            jax.ShapeDtypeStruct(codes.shape, jnp.int32),
+            jax.ShapeDtypeStruct((members, 2, capacity), jnp.int32),
+        ),
+        in_specs=[vmem],
+        out_specs=(vmem, vmem),
+        scratch_shapes=[
+            pltpu.VMEM((num_peers, 2, capacity), jnp.int32),
+            pltpu.SemaphoreType.DMA,
+            pltpu.SemaphoreType.DMA,
+            pltpu.SemaphoreType.DMA,
+        ],
+        compiler_params=pltpu.CompilerParams(
+            collective_id=1, has_side_effects=True, vmem_limit_bytes=60 * 2**20
+        ),
+        name="ask",
+    )(codes)
 
 
 def block_of(count, limit):
@@ -79,8 +200,11 @@
     )(slot_ids[None, :], vectors)
 
 
-def exchange(first, second, first_ids, second_ids, second_quant, ema_sums, decay, slabs, num_peers):
+def exchange(first, flat, answer, slots, first_ids, second_ids, second_quant, ema_sums, decay, slabs, num_peers):
     members, capacity, part = first.shape
+    tokens, channels = flat.shape
+    total = num_peers * capacity
+    pick_block, pack_block = block_of(tokens, 256), capacity * block_of(num_peers, 4)
     code_rows = ema_sums.shape[1]
     amount = members * capacity
     block = code_rows
@@ -90,7 +214,10 @@
 
     def kernel(
         first_ref,
-        second_ref,
+        flat_ref,
+        answer_ref,
+        place_ref,
+        slot_ref,
         first_id_ref,
         second_id_ref,
         quant_ref,
@@ -98,6 +225,8 @@
         decay_ref,
         sums_ref,
         error_ref,
+        residual,
+        second_out,
         first_in,
         second_in,
         squares,
@@ -145,9 +274,30 @@
             pltpu.make_async_copy(most, most, sems.at[which]).wait()
 
         send(first_ref, first_in, 0)
-        send(second_ref, second_in, 1)
         own(first_ref, first_in, 0).start()
-        own(second_ref, second_in, 1).start()
+
+        @pl.loop(0, tokens // pick_block)
+        def _(step):
+            here = pl.ds(pl.multiple_of(step * pick_block, pick_block), pick_block)
+            places = lax.broadcasted_iota(jnp.int32, (pick_block, total), 1)
+            hot = jnp.where(places == place_ref[here, :], 1.0, 0.0).astype(jnp.bfloat16)
+            quant = jnp.dot(hot, answer_ref[...], preferred_element_type=jnp.float32)
+            residual[here, :] = (flat_ref[here, :].astype(jnp.float32) - quant).astype(jnp.bfloat16)
+
+        @pl.loop(0, total // pack_block)
+        def _(step):
+            places = step * pack_block + lax.broadcasted_iota(jnp.int32, (pack_block, tokens), 0)
+            hot = jnp.where(places == slot_ref[...], 1.0, 0.0).astype(jnp.bfloat16)
+            rows = jnp.dot(hot, residual[...], preferred_element_type=jnp.float32)
+            rows = rows.astype(jnp.bfloat16)
+            count = pack_block // capacity
+            for slab in range(slabs):
+                second_out[pl.ds(slab * num_peers + step * count, count)] = rows[
+                    :, slab * part : (slab + 1) * part
+                ].reshape(count, capacity, part)
+
+        send(second_out, second_in, 1)
+        own(second_out, second_in, 1).start()
 
         def tally(which, id_ref, landing, begin, end):
             ids = id_ref[...]
@@ -166,7 +316,7 @@
         own(first_ref, first_in, 0).wait()
         finish(first_in, recv_sems, 0)
         tally(0, first_id_ref, first_in, 0, blocks)
-        own(second_ref, second_in, 1).wait()
+        own(second_out, second_in, 1).wait()
         finish(second_in, recv_sems, 1)
 
         @pl.loop(0, members)
@@ -191,11 +341,13 @@
             jax.ShapeDtypeStruct(ema_sums.shape, jnp.float32),
             jax.ShapeDtypeStruct((members, 1, capacity), jnp.float32),
         ),
-        in_specs=[vmem] * 6 + [pl.BlockSpec(memory_space=pltpu.SMEM)],
+        in_specs=[vmem] * 9 + [pl.BlockSpec(memory_space=pltpu.SMEM)],
         out_specs=(vmem, vmem),
         scratch_shapes=[
+            pltpu.VMEM(flat.shape, jnp.bfloat16),
             pltpu.VMEM(first.shape, jnp.bfloat16),
-            pltpu.VMEM(second.shape, jnp.bfloat16),
+            pltpu.VMEM(first.shape, jnp.bfloat16),
+            pltpu.VMEM(first.shape, jnp.bfloat16),
             pltpu.VMEM((members, 1, capacity), jnp.float32),
             pltpu.SemaphoreType.DMA((3,)),
             pltpu.SemaphoreType.DMA((3,)),
@@ -207,7 +359,10 @@
         name="exchange",
     )(
         first,
-        second,
+        flat,
+        answer,
+        slots[0][:, None],
+        slots[1][None, :],
         first_ids[None, :],
         second_ids[None, :],
         second_quant.reshape(members, capacity, part),
@@ -247,7 +402,6 @@
     amount = codes_first.size
     capacity = 2 * amount // num_peers
     total = num_peers * capacity
-    offset = lax.axis_index("height") * code_rows
     slab = lax.axis_index("tm")
     everyone = ("tm", "height")
 
@@ -259,21 +413,14 @@
     row_before = lax.ppermute(last_row, "height", peers)
     row_after = lax.ppermute(first_row, "height", [(j, i) for i, j in peers])
 
-    slots = slots_of(codes, num_peers, capacity, code_rows)
-    wanted = wanted_of(codes, slots, total).reshape(2, num_peers, capacity).swapaxes(0, 1)
-    wanted = jnp.broadcast_to(wanted[None], (slabs,) + wanted.shape).reshape(
-        slabs * num_peers, 2 * capacity
-    )
-    got = lax.all_to_all(wanted, everyone, split_axis=0, concat_axis=0, tiled=True)
-    got = got.reshape(slabs, num_peers, 2, capacity) - offset
+    slots, got = ask(codes, num_peers, slabs, capacity, code_rows)
+    got = got.reshape(slabs, num_peers, 2, capacity)
     mine = lax.dynamic_index_in_dim(got[:, :, 0], slab, 0, keepdims=False)
     answer = picked(mine.reshape(-1), codebooks[0]).reshape(num_peers, capacity, channels)
     answer = lax.all_to_all(answer, "height", split_axis=0, concat_axis=0, tiled=True)
 
     widened = latents.astype(jnp.float32)
-    normed = normalize(latents, norm_gain)
-    padded = jnp.concatenate([row_before, normed, row_after], axis=2)
-    hidden = convolve(padded, spatial_weight)
+    hidden = convolve(latents, norm_gain, row_before, row_after, spatial_weight)
     earlier = lax.ppermute(hidden, "tm", [(i, i + 1) for i in range(slabs - 1)])
     first_ids, second_ids = got[:, :, 0].reshape(-1), got[:, :, 1].reshape(-1)
     table = lax.dynamic_slice_in_dim(codebooks[1], slab * part, part, axis=1)
@@ -296,14 +443,12 @@
     encoded = (widened + mixed).astype(jnp.bfloat16)
     flat = encoded.reshape(-1, channels)
 
-    def packed(vectors, slot):
-        return pack(slot, vectors, total, slabs).reshape(slabs * num_peers, capacity, part)
-
-    first_quant = picked(slots[0], answer.reshape(total, channels))
-    residual = (flat.astype(jnp.float32) - first_quant.astype(jnp.float32)).astype(jnp.bfloat16)
+    packed = pack(slots[0], flat, total, slabs).reshape(slabs * num_peers, capacity, part)
     ema_sums_new, squares = exchange(
-        packed(flat, slots[0]),
-        packed(residual, slots[1]),
+        packed,
+        flat,
+        answer.reshape(total, channels),
+        slots,
         first_ids,
         second_ids,
         second_quant,

time: 227 us -> 214 us (0.943)
  Pallas kernels: 127 us -> 146 us
  matrix products: 33.6 us -> 15.4 us
  starting transfers between devices: 20.8 us -> 11.4 us
  waiting for transfers between devices: 17 us -> 12.1 us
  local copies, waits for them, and re-layouts: 6.54 us -> 11.3 us
  other arithmetic: 20.3 us -> 16.7 us
    pallas_call x0 -> x2, Pallas kernels: none -> 23 us  [the longest x1 16.9 us: ask(): pl.pallas_call(kernel, out_shape=(jax.ShapeDtypeStruct(codes.shape, jnp.i...]
    conv_general_dilated x1 -> x0, matrix products: 13.8 us -> none  [convolve(): lax.conv_general_dilated(padded.reshape(clips * frames, rows, width, chan...]
    all_to_all x1 -> x0, starting transfers between devices: 7.32 us -> none  [body(): lax.all_to_all(wanted, everyone, split_axis=0, concat_axis=0, tiled=True)]
    pallas_call x2 -> x1, Pallas kernels: 10.1 us -> 4.96 us  [pack(): pl.pallas_call(kernel, grid=(total // block,), out_shape=jax.ShapeDtypeSt...]
    dot_general x3 -> x2, matrix products: 19.2 us -> 15.4 us  [picked(): jnp.dot(rows_by(ids, table.shape[0]), table, preferred_element_type=jnp.f...]
    ppermute x1, waiting for transfers between devices: 15.3 us -> 12.1 us  [body(): earlier = lax.ppermute(hidden, 'tm', [(i, i + 1) for i in range(slabs - 1)])]
    unnamed x22 -> x23, local copies, waits for them, and re-layouts: 4.52 us -> 6.84 us
  transfers between devices with their start and end apart: 5 -> 4, of which waited for: 2 -> 1; matrix products, arithmetic and copies ran while one was open for 18% -> 13% of each run, Pallas kernels for 2% -> 13%
where the time goes in v2:
time: 214 us
  Pallas kernels  146 us (68%)
  other arithmetic  16.7 us (8%)
  matrix products  15.4 us (7%)
  waiting for transfers between devices  12.1 us (6%)
  starting transfers between devices  11.4 us (5%)
  local copies, waits for them, and re-layouts  11.3 us (5%)
    pallas_call x1, Pallas kernels, exchange(): pl.pallas_call(kernel, out_shape=(jax.ShapeDtypeStruct(ema_sums.shape, jn...  118 us
    pallas_call x1, Pallas kernels, ask(): pl.pallas_call(kernel, out_shape=(jax.ShapeDtypeStruct(codes.shape, jnp.i...  16.9 us
    dot_general x2, matrix products, picked(): jnp.dot(rows_by(ids, table.shape[0]), table, preferred_element_type=jnp.f...  15.4 us
    ppermute x1, waiting for transfers between devices, body(): earlier = lax.ppermute(hidden, 'tm', [(i, i + 1) for i in range(slabs - 1)])  12.1 us
    unnamed x23, local copies, waits for them, and re-layouts  6.84 us
    reduce_sum x2, other arithmetic, body(): jnp.sum((marks == ids[None, :]).astype(jnp.float32), axis=1)  6.77 us
    pallas_call x1, Pallas kernels, convolve(): pl.pallas_call(body, grid=(images,), out_shape=jax.ShapeDtypeStruct((imag...  6.06 us
    pallas_call x1, Pallas kernels, pack(): pl.pallas_call(kernel, grid=(total // block,), out_shape=jax.ShapeDtypeSt...  4.96 us
  transfers between devices with their start and end apart: 4, of which 1 were waited for; matrix products, arithmetic and copies ran while one was open for 13% of the time, Pallas kernels for 13%

profile of v2, /device:TPU:0, one launch (start us, length us, event | category | flops | bytes accessed | tf_op | source)
XLA Modules:
  0.0 213.7 jit_solution(13124225932710400921)
XLA Ops:
  0.6 1.5 fusion.11
  2.1 1.3 pad_add_fusion.code_ref
  3.4 1.5 fusion.13
  5.0 2.4 %collective-permute-start = (bf16[2,2,1,128,512]{4,3,2,1,0:T(8,128)(2,1)S(1)}, bf16[2,2,1,128,512]{4,3,2,1,0:T(8,128)(2,1)S(1)}, u32[]{:S(2)}, u32[]{:S(2)}) collective-permute-start(bf16[2,2,1,128,512]{4,3,2,1,0:T(8,128)(2,1)S(1)} %get-tuple-element.15), channel_id=1, source_target_pairs={{0,1},{1,2},{2,3},{3,4},{4,5},{5,6},{6,7},{7,8},{8,9},{9,10},{10,1... | collective-permute-start | bytes 1572872 | tf_op jit(solution)/shard_map/ppermute | solution.py:413
  7.4 1.3 collective-permute-start.1
  8.7 16.9 %ask.1 = (s32[2,1024]{1,0:T(2,128)}, s32[32,2,128]{2,1,0:T(2,128)}) custom-call(s32[2,1024]{1,0:T(2,128)} %pad_add_fusion.code_ref), custom_call_target="tpu_custom_call" | custom-call | tf_op jit(solution)/shard_map/ask/pallas_call | solution.py:145
  25.7 0.9 fusion.18
  26.6 7.4 %fusion.5 = bf16[2048,512]{1,0:T(8,128)(2,1)} fusion(s32[2048]{0:T(1024)S(1)} %dynamic-slice_bitcast_fusion, bf16[2,2048,512]{2,1,0:T(8,128)(2,1)} %param.14), kind=kOutput, calls=%fused_computation.13 | convolution fusion | flops 4300210176 | bytes 4202496 | tf_op jit(solution)/shard_map/dot_general | solution.py:379
  34.0 0.0 copy-start.1
  34.0 4.9 %all-to-all-start = ((bf16[16,128,512]{2,1,0:T(8,128)(2,1)}), bf16[16,128,512]{2,1,0:T(8,128)(2,1)}, u32[]{:S(2)}, u32[]{:S(2)}) async-start(bf16[16,128,512]{2,1,0:T(8,128)(2,1)} %bitcast.48), calls=%async_computation | async-start | bytes 4194304 | tf_op jit(solution)/shard_map/all_to_all | solution.py:420
  38.9 0.6 fusion.19
  39.5 3.4 %convert_reduce_fusion.1 = f32[2048]{0:T(1024)S(1)} fusion(s32[4096]{0:T(1024)S(1)} %bitcast.52), kind=kLoop, calls=%fused_computation.3 | loop fusion | flops 25163776 | bytes 24576 | tf_op jit(solution)/shard_map/reduce_sum | solution.py:431
  42.9 3.4 %convert_reduce_fusion = f32[2048]{0:T(1024)S(1)} fusion(s32[4096]{0:T(1024)S(1)} %bitcast.54), kind=kLoop, calls=%fused_computation.1 | loop fusion | flops 25163776 | bytes 24576 | tf_op jit(solution)/shard_map/reduce_sum | solution.py:431
  46.3 0.7 fusion.16
  47.0 0.0 collective-permute-done
  47.0 0.0 collective-permute-done.1
  47.0 0.0 copy-start.2
  47.0 2.3 %copy-done.2 = bf16[3,3,512,512]{3,2,1,0:T(8,128)(2,1)S(1)} copy-done((bf16[3,3,512,512]{3,2,1,0:T(8,128)(2,1)S(1)}, bf16[3,3,512,512]{3,2,1,0:T(8,128)(2,1)}, u32[]{:S(2)}) %copy-start.2) | copy-done | bytes 4718616
  49.4 6.1 %convolve.1 = bf16[4,2,128,512]{3,2,1,0:T(8,128)(2,1)S(1)} custom-call(bf16[4,2,128,512]{3,2,1,0:T(8,128)(2,1)S(1)} %bitcast.40, f32[1,512]{1,0:T(1,128)S(1)} %bitcast.43, bf16[4,128,512]{2,1,0:T(8,128)(2,1)S(1)} %bitcast.44, bf16[4,128,512]{2,1,0:T(8,128)(2,1)S(1)} %bitcast.45, bf16[3,3,512,512]{3,2,1,0:T(8,128)(2,1)S(1)} %copy-done.2), custom_call_target="tpu_custom_call" | custom-call | flops 4831838208 | bytes 6815744 | tf_op jit(solution)/shard_map/convolve/pallas_call | solution.py:39
  55.4 2.8 %collective-permute-start.2 = (bf16[2,2,2,128,512]{4,3,2,1,0:T(8,128)(2,1)S(1)}, bf16[2,2,2,128,512]{4,3,2,1,0:T(8,128)(2,1)S(1)}, u32[]{:S(2)}, u32[]{:S(2)}) collective-permute-start(bf16[2,2,2,128,512]{4,3,2,1,0:T(8,128)(2,1)S(1)} %bitcast.41), channel_id=1, source_target_pairs={{0,16},{1,17},{2,18},{3,19},{4,20},{5,21},{6,22},{7,23},{8,24},{9,... | collective-permute-start | bytes 3145736 | tf_op jit(solution)/shard_map/ppermute | solution.py:424
  58.3 1.5 slice.45
  59.7 1.0 copy.20.place_ref
  60.7 8.1 %fusion.4 = bf16[4096,256]{1,0:T(8,128)(2,1)} fusion(s32[4096]{0:T(1024)S(1)} %bitcast.55, bf16[1,2048,512]{2,1,0:T(8,128)(2,1)} %slice.45, s32[]{:T(128)S(6)} %select_n.11), kind=kOutput, calls=%fused_computation.12 | convolution fusion | flops 4304404480 | bytes 3162116 | tf_op jit(solution)/shard_map/dot_general | solution.py:379
  68.8 12.1 %collective-permute-done.2 = bf16[2,2,2,128,512]{4,3,2,1,0:T(8,128)(2,1)S(1)} collective-permute-done((bf16[2,2,2,128,512]{4,3,2,1,0:T(8,128)(2,1)S(1)}, bf16[2,2,2,128,512]{4,3,2,1,0:T(8,128)(2,1)S(1)}, u32[]{:S(2)}, u32[]{:S(2)}) %collective-permute-start.2) | collective-permute-done | bytes 1048608 | tf_op jit(solution)/shard_map/ppermute | solution.py:424
  80.8 1.7 add_convert_fusion
  82.6 5.0 %pack.1 = bf16[2,2048,256]{2,1,0:T(8,128)(2,1)} custom-call(s32[1,1024]{1,0:T(1,128)} %get-tuple-element.29.slot_ref, bf16[1024,512]{1,0:T(8,128)(2,1)} %bitcast.46), custom_call_target="tpu_custom_call" | custom-call | flops 2147483648 | bytes 6291456 | tf_op jit(solution)/shard_map/pack/pallas_call | solution.py:187
  87.5 117.9 %exchange.1 = (f32[2,2048,256]{2,1,0:T(8,128)}, f32[32,1,128]{2,1,0:T(1,128)}) custom-call(bf16[32,128,256]{2,1,0:T(8,128)(2,1)} %bitcast.50, bf16[1024,512]{1,0:T(8,128)(2,1)} %bitcast.47, bf16[2048,512]{1,0:T(8,128)(2,1)} %bitcast.21.answer_ref, s32[1024,1]{1,0:T(8,128)} %copy.20.place_ref, s32[1,1024]{1,0:T(1,128)} %get-tuple-element.27.slot_ref, ...), custom_call_target="tpu_custom_call" | custom-call | tf_op jit(solution)/shard_map/exchange/pallas_call | solution.py:338
  205.5 0.5 broadcast.54
  206.0 1.4 reduce.5
  207.4 1.2 select_reduce_fusion
  208.6 0.6 broadcast_multiply_fusion
  209.2 4.5 %copy.24 = f32[2,2048,256]{2,1,0:T(8,128)} copy(f32[2,2048,256]{2,1,0:T(8,128)} %get-tuple-element.39) | data formatting | bytes 8388608
  (26 shorter events, 0.1 us)
Async XLA Ops:
  5.0 42.0 %collective-permute-start = (bf16[2,2,1,128,512]{4,3,2,1,0:T(8,128)(2,1)S(1)}, bf16[2,2,1,128,512]{4,3,2,1,0:T(8,128)(2,1)S(1)}, u32[]{:S(2)}, u32[]{:S(2)}) collective-permute-start(bf16[2,2,1,128,512]{4,3,2,1,0:T(8,128)(2,1)S(1)} %get-tuple-element.15), channel_id=1, source_target_pairs={{0,1},{1,2},{2,3},{3,4},{4,5},{5,6},{6,7},{7,8},{8,9},{9,10},{10,1... | collective-permute-start | bytes 1572872 | tf_op jit(solution)/shard_map/ppermute | solution.py:413
  7.4 39.6 %collective-permute-start.1 = (bf16[2,2,1,128,512]{4,3,2,1,0:T(8,128)(2,1)S(1)}, bf16[2,2,1,128,512]{4,3,2,1,0:T(8,128)(2,1)S(1)}, u32[]{:S(2)}, u32[]{:S(2)}) collective-permute-start(bf16[2,2,1,128,512]{4,3,2,1,0:T(8,128)(2,1)S(1)} %get-tuple-element.16), channel_id=1, source_target_pairs={{1,0},{2,1},{3,2},{4,3},{5,4},{6,5},{7,6},{8,7},{9,8},{10,9},{11,1... | collective-permute-start | bytes 1572872 | tf_op jit(solution)/shard_map/ppermute | solution.py:414
  26.5 13.0 %copy-start.4 = (s32[2,16,1,128]{3,2,1,0:T(1,128)}, s32[2,16,1,128]{3,2,1,0:T(1,128)S(1)}, u32[]{:S(2)}) copy-start(s32[2,16,1,128]{3,2,1,0:T(1,128)S(1)} %get-tuple-element.25) | copy-start | bytes 49156
  26.5 34.2 %copy-start.5 = (s32[2,16,1,128]{3,2,1,0:T(1,128)}, s32[2,16,1,128]{3,2,1,0:T(1,128)S(1)}, u32[]{:S(2)}) copy-start(s32[2,16,1,128]{3,2,1,0:T(1,128)S(1)} %get-tuple-element.26) | copy-start | bytes 49156
  34.0 5.0 %copy-start.8 = (s32[2,1024]{1,0:T(2,128)S(1)}, s32[2,1024]{1,0:T(2,128)}, u32[]{:S(2)}) copy-start(s32[2,1024]{1,0:T(2,128)} %get-tuple-element.14) | copy-start | bytes 24580
  34.0 12.3 %copy-start.10 = (f32[2]{0:T(128)S(1)}, f32[2]{0:T(128)}, u32[]{:S(2)}) copy-start(f32[2]{0:T(128)} %decay_ref.1) | copy-start | bytes 28
  34.0 12.4 %copy-start.7 = (f32[2,2048]{1,0:T(2,128)S(1)}, f32[2,2048]{1,0:T(2,128)}, u32[]{:S(2)}) copy-start(f32[2,2048]{1,0:T(2,128)} %param.15) | copy-start | bytes 49156
  34.0 13.1 %copy-start = (bf16[2,2,2,128,512]{4,3,2,1,0:T(8,128)(2,1)S(1)}, bf16[2,2,2,128,512]{4,3,2,1,0:T(8,128)(2,1)}, u32[]{:S(2)}) copy-start(bf16[2,2,2,128,512]{4,3,2,1,0:T(8,128)(2,1)} %param.10) | copy-start | bytes 3145732
  34.0 13.1 %copy-start.1 = (f32[512]{0:T(512)S(1)}, f32[512]{0:T(512)}, u32[]{:S(2)}) copy-start(f32[512]{0:T(512)} %param.11) | copy-start | bytes 6148
  34.0 53.5 %all-to-all-start = ((bf16[16,128,512]{2,1,0:T(8,128)(2,1)}), bf16[16,128,512]{2,1,0:T(8,128)(2,1)}, u32[]{:S(2)}, u32[]{:S(2)}) async-start(bf16[16,128,512]{2,1,0:T(8,128)(2,1)} %bitcast.48), calls=%async_computation | async-start | bytes 4194304 | tf_op jit(solution)/shard_map/all_to_all | solution.py:420
  47.0 2.3 %copy-start.2 = (bf16[3,3,512,512]{3,2,1,0:T(8,128)(2,1)S(1)}, bf16[3,3,512,512]{3,2,1,0:T(8,128)(2,1)}, u32[]{:S(2)}) copy-start(bf16[3,3,512,512]{3,2,1,0:T(8,128)(2,1)} %weight_ref.1) | copy-start | bytes 14155780
  49.4 8.9 %copy-start.9 = (f32[3,512]{1,0:T(4,128)S(1)}, f32[3,512]{1,0:T(4,128)}, u32[]{:S(2)}) copy-start(f32[3,512]{1,0:T(4,128)} %param.13) | copy-start | bytes 18436
  49.4 8.9 %copy-start.3 = (bf16[2,2048,512]{2,1,0:T(8,128)(2,1)S(1)}, bf16[2,2048,512]{2,1,0:T(8,128)(2,1)}, u32[]{:S(2)}) copy-start(bf16[2,2048,512]{2,1,0:T(8,128)(2,1)} %param.14) | copy-start | bytes 12582916
  55.4 25.4 %collective-permute-start.2 = (bf16[2,2,2,128,512]{4,3,2,1,0:T(8,128)(2,1)S(1)}, bf16[2,2,2,128,512]{4,3,2,1,0:T(8,128)(2,1)S(1)}, u32[]{:S(2)}, u32[]{:S(2)}) collective-permute-start(bf16[2,2,2,128,512]{4,3,2,1,0:T(8,128)(2,1)S(1)} %bitcast.41), channel_id=1, source_target_pairs={{0,16},{1,17},{2,18},{3,19},{4,20},{5,21},{6,22},{7,23},{8,24},{9,... | collective-permute-start | bytes 3145736 | tf_op jit(solution)/shard_map/ppermute | solution.py:424
  87.5 119.9 %copy-start.6 = (s32[1,1024]{1,0:T(1,128)S(1)}, s32[1,1024]{1,0:T(1,128)}, u32[]{:S(2)}) copy-start(s32[1,1024]{1,0:T(1,128)} %get-tuple-element.27.slot_ref) | copy-start | bytes 12292

commit v3 on v2

v3 whole, which is shorter than its diff:
```python
import jax
import jax.numpy as jnp
from jax import lax
from jax.experimental import pallas as pl
from jax.experimental.pallas import tpu as pltpu
from jax.sharding import PartitionSpec as P


def normalize(values, norm_gain):
    widened = values.astype(jnp.float32)
    inverse = lax.rsqrt(jnp.mean(widened * widened, axis=-1, keepdims=True) + 1e-06)
    return (widened * inverse * norm_gain).astype(jnp.bfloat16)


def ask(codes, num_peers, slabs, capacity, code_rows):
    amount = codes.shape[1]
    members = slabs * num_peers
    total = num_peers * capacity

    def kernel(code_ref, slot_ref, ids_ref, outgoing, local_sem, send_sem, recv_sem):
        me_row = lax.axis_index("height")
        me = lax.axis_index("tm") * num_peers + me_row

        def peer_of(step):
            peer = lax.rem(me + step, members)
            row = lax.rem(peer, num_peers)
            return row, {"tm": peer // num_peers, "height": row}

        barrier = pltpu.get_barrier_semaphore()

        @pl.loop(1, members)
        def _(step):
            _, target = peer_of(step)
            pl.semaphore_signal(
                barrier, inc=1, device_id=target, device_id_type=pl.DeviceIdType.MESH
            )

        owners = lax.broadcasted_iota(jnp.int32, (num_peers, amount), 0)
        later = lax.broadcasted_iota(jnp.int32, (amount, amount), 1)
        sooner = lax.broadcasted_iota(jnp.int32, (amount, amount), 0)
        order = jnp.where(sooner < later, 1.0, 0.0).astype(jnp.bfloat16)
        for which in range(2):
            code = code_ref[which : which + 1, :]
            local = code - owners * code_rows
            mark = jnp.where((local >= 0) & (local < code_rows), 1.0, 0.0)
            before = jnp.dot(
                mark.astype(jnp.bfloat16), order, preferred_element_type=jnp.float32
            )
            place = mark * (before + (owners * capacity).astype(jnp.float32))
            slot = jnp.sum(place, axis=0, keepdims=True)
            local = jnp.sum(jnp.where(mark > 0.0, local, 0), axis=0, keepdims=True)
            slot_ref[which : which + 1, :] = slot.astype(jnp.int32)
            high = (local // 256).astype(jnp.float32)
            low = (local % 256).astype(jnp.float32)
            kind = lax.broadcasted_iota(jnp.int32, (16, amount), 0)
            digits = jnp.where(kind == 0, high, jnp.where(kind == 1, low, 1.0))
            digits = digits.astype(jnp.bfloat16)
            places = lax.broadcasted_iota(jnp.int32, (total, amount), 0).astype(jnp.float32)
            hot = jnp.where(places == slot, 1.0, 0.0).astype(jnp.bfloat16)
            found = lax.dot_general(
                digits, hot, (((1,), (1,)), ((), ())), preferred_element_type=jnp.float32
            )
            wanted = found[0:1] * 256.0 + found[1:2] + found[2:3] - 1.0
            wanted = wanted.astype(jnp.int32)
            for row in range(num_peers):
                outgoing[row, which : which + 1, :] = wanted[
                    :, row * capacity : (row + 1) * capacity
                ]

        pl.semaphore_wait(barrier, members - 1)

        @pl.loop(1, members)
        def _(step):
            row, target = peer_of(step)
            pltpu.make_async_remote_copy(
                src_ref=outgoing.at[row],
                dst_ref=ids_ref.at[me],
                send_sem=send_sem,
                recv_sem=recv_sem,
                device_id=target,
                device_id_type=pl.DeviceIdType.MESH,
            ).start()

        own = pltpu.make_async_copy(outgoing.at[me_row], ids_ref.at[me], local_sem)
        own.start()
        own.wait()
        most = ids_ref.at[pl.ds(0, members - 1)]
        pltpu.make_async_copy(most, most, recv_sem).wait()
        pltpu.make_async_copy(most, most, send_sem).wait()

    vmem = pl.BlockSpec(memory_space=pltpu.VMEM)
    return pl.pallas_call(
        kernel,
        out_shape=(
            jax.ShapeDtypeStruct(codes.shape, jnp.int32),
            jax.ShapeDtypeStruct((members, 2, capacity), jnp.int32),
        ),
        in_specs=[vmem],
        out_specs=(vmem, vmem),
        scratch_shapes=[
            pltpu.VMEM((num_peers, 2, capacity), jnp.int32),
            pltpu.SemaphoreType.DMA,
            pltpu.SemaphoreType.DMA,
            pltpu.SemaphoreType.DMA,
        ],
        compiler_params=pltpu.CompilerParams(
            collective_id=1, has_side_effects=True, vmem_limit_bytes=60 * 2**20
        ),
        name="ask",
    )(codes)


def block_of(count, limit):
    block = count
    while block > limit and block % 2 == 0:
        block //= 2
    return block


def main(
    latents,
    norm_gain,
    row_before,
    row_after,
    spatial_weight,
    temporal_weight,
    codebooks,
    table,
    got,
    slots,
    slabs,
    num_peers,
    capacity,
):
    clips, frames, rows, width, channels = latents.shape
    images, pixels = clips * frames, rows * width
    tokens = images * pixels
    part = channels // slabs
    members, total = slabs * num_peers, num_peers * capacity
    amount = members * capacity
    code_rows = codebooks.shape[1]
    group = block_of(num_peers, 4)
    span = group * capacity
    pick_block = block_of(tokens, 256)
    block = code_rows
    while block * amount > 2**20 and block % 2 == 0:
        block //= 2
    blocks = code_rows // block

    def kernel(
        latent_ref,
        gain_ref,
        before_ref,
        after_ref,
        temporal_ref,
        table_ref,
        first_id_ref,
        second_id_ref,
        first_slot_ref,
        second_slot_ref,
        weight_hbm,
        book_hbm,
        sums_ref,
        error_ref,
        count_ref,
        weight_ref,
        book_ref,
        served,
        answer,
        hidden,
        earlier,
        flat,
        residual,
        first_out,
        second_out,
        first_in,
        second_in,
        quants,
        squares,
        load_sems,
        local_sems,
        send_sems,
        recv_sems,
    ):
        me_slab = lax.axis_index("tm")
        me_row = lax.axis_index("height")
        me = me_slab * num_peers + me_row
        load_book = pltpu.make_async_copy(book_hbm.at[0], book_ref, load_sems.at[0])
        load_weight = pltpu.make_async_copy(weight_hbm, weight_ref, load_sems.at[1])
        load_book.start()
        load_weight.start()

        def peer_of(step):
            peer = lax.rem(me + step, members)
            return peer, {"tm": peer // num_peers, "height": lax.rem(peer, num_peers)}

        def push(source, landing, which, target):
            return pltpu.make_async_remote_copy(
                src_ref=source,
                dst_ref=landing,
                send_sem=send_sems.at[which],
                recv_sem=recv_sems.at[which],
                device_id=target,
                device_id_type=pl.DeviceIdType.MESH,
            )

        def send(source, landing, which):
            @pl.loop(1, members)
            def _(step):
                peer, target = peer_of(step)
                push(source.at[peer], landing.at[me], which, target).start()

        def own(source, landing, which, at):
            return pltpu.make_async_copy(source.at[at], landing.at[at], local_sems.at[which])

        def rows_at(ids, table):
            marks = lax.broadcasted_iota(jnp.int32, (table.shape[0], ids.shape[1]), 0)
            hot = jnp.where(marks == ids, 1.0, 0.0).astype(jnp.bfloat16)
            return lax.dot_general(
                hot, table, (((0,), (0,)), ((), ())), preferred_element_type=jnp.float32
            )

        def finish(landing, sems, which, count):
            most = landing.at[pl.ds(0, count)]
            pltpu.make_async_copy(most, most, sems.at[which]).wait()

        barrier = pltpu.get_barrier_semaphore()

        @pl.loop(1, members)
        def _(step):
            _, target = peer_of(step)
            pl.semaphore_signal(
                barrier, inc=1, device_id=target, device_id_type=pl.DeviceIdType.MESH
            )

        load_book.wait()
        pl.semaphore_wait(barrier, members - 1)

        @pl.loop(0, num_peers // group)
        def _(step):
            base = lax.rem(me_row // group + step, num_peers // group) * group
            here = pl.ds(pl.multiple_of(me_slab * total + base * capacity, span), span)
            found = rows_at(first_id_ref[:, here], book_ref[...])
            found = found.astype(jnp.bfloat16).reshape(group, capacity, channels)
            served[pl.ds(base, group)] = found

            @pl.loop(0, group)
            def _(offset):
                peer = base + offset

                @pl.when(peer != me_row)
                def _():
                    target = {"tm": me_slab, "height": peer}
                    push(served.at[peer], answer.at[me_row], 3, target).start()

        own(served, answer, 3, me_row).start()
        load_weight.wait()
        last_slab = me_slab + 1 >= slabs
        column = lax.rem(lax.broadcasted_iota(jnp.int32, (pixels, channels), 0), width)

        def forward(image):
            return push(
                hidden.at[image],
                earlier.at[image],
                4,
                {"tm": lax.rem(me_slab + 1, slabs), "height": me_row},
            )

        @pl.loop(0, images)
        def _(image):
            normed = normalize(latent_ref[image], gain_ref[...])
            taps = jnp.concatenate([before_ref[image], normed, after_ref[image]], axis=0)
            windows = [taps[row * width : (row + rows) * width] for row in range(3)]

            def tap(col):
                added = jnp.dot(windows[0], weight_ref[0, col], preferred_element_type=jnp.float32)
                for row in (1, 2):
                    added += jnp.dot(
                        windows[row], weight_ref[row, col], preferred_element_type=jnp.float32
                    )
                return added

            summed = tap(1)
            summed += jnp.where(column == 0, 0.0, pltpu.roll(tap(0), 1, 0))
            summed += jnp.where(column == width - 1, 0.0, pltpu.roll(tap(2), pixels - 1, 0))
            hidden[image] = (summed / (1.0 + jnp.exp(-summed))).astype(jnp.bfloat16)

            @pl.when(jnp.logical_not(last_slab))
            def _():
                forward(image).start()

        @pl.loop(0, members // group)
        def _(step):
            here = pl.ds(pl.multiple_of(step * span, span), span)
            found = rows_at(second_id_ref[:, here], table_ref[...])
            found = found.astype(jnp.bfloat16).reshape(group, capacity, part)
            quants[pl.ds(step * group, group)] = found

        @pl.when(me_slab > 0)
        def _():
            finish(earlier, recv_sems, 4, images)

        @pl.when(me_slab == 0)
        def _():
            earlier[...] = jnp.zeros(earlier.shape, jnp.bfloat16)

        for image in range(images):
            clip, frame = image // frames, image % frames
            mixed = jnp.zeros((pixels, channels), jnp.float32)
            for tap in range(3):
                at = frame - 2 + tap
                frame_ref = hidden if at >= 0 else earlier
                value = frame_ref[clip * frames + at % frames].astype(jnp.float32)
                mixed = mixed + temporal_ref[tap : tap + 1, :] * value
            encoded = latent_ref[image].astype(jnp.float32) + mixed
            flat[image * pixels : (image + 1) * pixels, :] = encoded.astype(jnp.bfloat16)

        def pack(slot_ref, vectors, out):
            @pl.loop(0, num_peers // group)
            def _(step):
                places = step * span + lax.broadcasted_iota(jnp.int32, (span, tokens), 0)
                hot = jnp.where(places == slot_ref[...], 1.0, 0.0).astype(jnp.bfloat16)
                packed = jnp.dot(hot, vectors[...], preferred_element_type=jnp.float32)
                packed = packed.astype(jnp.bfloat16)
                for slab in range(slabs):
                    out[pl.ds(slab * num_peers + step * group, group)] = packed[
                        :, slab * part : (slab + 1) * part
                    ].reshape(group, capacity, part)

        pack(first_slot_ref, flat, first_out)
        send(first_out, first_in, 0)
        own(first_out, first_in, 0, me).start()
        own(served, answer, 3, me_row).wait()
        finish(answer, recv_sems, 3, num_peers - 1)

        @pl.loop(0, tokens // pick_block)
        def _(step):
            here = pl.ds(pl.multiple_of(step * pick_block, pick_block), pick_block)
            quant = rows_at(first_slot_ref[:, here], answer[...].reshape(total, channels))
            residual[here, :] = (flat[here, :].astype(jnp.float32) - quant).astype(jnp.bfloat16)

        pack(second_slot_ref, residual, second_out)
        send(second_out, second_in, 1)
        own(second_out, second_in, 1, me).start()

        def tally(which, id_ref, landing, begin, end):
            ids = id_ref[...]

            @pl.loop(begin, end)
            def _(step):
                start = pl.multiple_of(step * block, block)
                places = start + lax.broadcasted_iota(jnp.int32, (block, amount), 0)
                hot = jnp.where(places == ids, 1.0, 0.0).astype(jnp.bfloat16)
                vectors = landing[...].reshape(amount, part)
                sums_ref[which, pl.ds(start, block), :] = jnp.dot(
                    hot, vectors, preferred_element_type=jnp.float32
                )

        for which, id_ref in ((0, first_id_ref), (1, second_id_ref)):
            ids = id_ref[...]

            @pl.loop(0, blocks)
            def _(step):
                marks = step * block + lax.broadcasted_iota(jnp.int32, (block, amount), 0)
                hot = jnp.where(marks == ids, 1.0, 0.0)
                count_ref[which, step] = jnp.sum(hot, axis=1)[None, :]

        own(first_out, first_in, 0, me).wait()
        finish(first_in, recv_sems, 0, members - 1)
        tally(0, first_id_ref, first_in, 0, blocks)
        own(second_out, second_in, 1, me).wait()
        finish(second_in, recv_sems, 1, members - 1)

        @pl.loop(0, members)
        def _(source):
            leftover = second_in[source].astype(jnp.float32) - quants[source].astype(jnp.float32)
            squares[source] = jnp.sum(leftover * leftover, axis=1)[None, :]

        tally(1, second_id_ref, second_in, 0, 1)
        send(squares, error_ref, 2)
        own(squares, error_ref, 2, me).start()
        tally(1, second_id_ref, second_in, 1, blocks)
        own(squares, error_ref, 2, me).wait()
        finish(error_ref, recv_sems, 2, members - 1)
        finish(first_in, send_sems, 0, members - 1)
        finish(second_in, send_sems, 1, members - 1)
        finish(error_ref, send_sems, 2, members - 1)
        finish(answer, send_sems, 3, num_peers - 1)

        @pl.when(jnp.logical_not(last_slab))
        def _():
            finish(hidden, send_sems, 4, images)

    vmem, anywhere = pl.BlockSpec(memory_space=pltpu.VMEM), pl.BlockSpec(memory_space=pl.ANY)
    bf16 = jnp.bfloat16
    pieces = (members, capacity, part)
    first_ids, second_ids = got[:, 0].reshape(-1), got[:, 1].reshape(-1)
    return pl.pallas_call(
        kernel,
        out_shape=(
            jax.ShapeDtypeStruct((2, code_rows, part), jnp.float32),
            jax.ShapeDtypeStruct((members, 1, capacity), jnp.float32),
            jax.ShapeDtypeStruct((2, blocks, 1, block), jnp.float32),
        ),
        in_specs=[vmem] * 10 + [anywhere] * 2,
        out_specs=(vmem, vmem, vmem),
        scratch_shapes=[
            pltpu.VMEM(spatial_weight.shape, bf16),
            pltpu.VMEM((code_rows, channels), bf16),
            pltpu.VMEM((num_peers, capacity, channels), bf16),
            pltpu.VMEM((num_peers, capacity, channels), bf16),
            pltpu.VMEM((images, pixels, channels), bf16),
            pltpu.VMEM((images, pixels, channels), bf16),
            pltpu.VMEM((tokens, channels), bf16),
            pltpu.VMEM((tokens, channels), bf16),
            pltpu.VMEM(pieces, bf16),
            pltpu.VMEM(pieces, bf16),
            pltpu.VMEM(pieces, bf16),
            pltpu.VMEM(pieces, bf16),
            pltpu.VMEM(pieces, bf16),
            pltpu.VMEM((members, 1, capacity), jnp.float32),
            pltpu.SemaphoreType.DMA((2,)),
            pltpu.SemaphoreType.DMA((4,)),
            pltpu.SemaphoreType.DMA((5,)),
            pltpu.SemaphoreType.DMA((5,)),
        ],
        compiler_params=pltpu.CompilerParams(
            collective_id=0, has_side_effects=True, vmem_limit_bytes=60 * 2**20
        ),
        name="main",
    )(
        latents.reshape(images, pixels, channels),
        norm_gain[None, :],
        row_before.reshape(images, width, channels),
        row_after.reshape(images, width, channels),
        temporal_weight,
        table,
        first_ids[None, :],
        second_ids[None, :],
        slots[0][None, :],
        slots[1][None, :],
        spatial_weight,
        codebooks,
    )


def body(
    latents,
    norm_gain,
    spatial_weight,
    temporal_weight,
    codebooks,
    ema_counts,
    ema_sums,
    decay,
    codes_first,
    codes_second,
):
    channels = latents.shape[-1]
    num_peers = lax.axis_size("height")
    slabs = lax.axis_size("tm")
    part = channels // slabs
    code_rows = codebooks.shape[1]
    amount = codes_first.size
    capacity = 2 * amount // num_peers
    total = num_peers * capacity

    peers = [(i, i + 1) for i in range(num_peers - 1)]
    first_row = normalize(latents[:, :, :1], norm_gain)
    last_row = normalize(latents[:, :, -1:], norm_gain)
    codes = jnp.stack([codes_first.reshape(-1), codes_second.reshape(-1)])
    first_row, last_row, codes = lax.optimization_barrier((first_row, last_row, codes))
    row_before = lax.ppermute(last_row, "height", peers)
    row_after = lax.ppermute(first_row, "height", [(j, i) for i, j in peers])

    slots, got = ask(codes, num_peers, slabs, capacity, code_rows)
    table = lax.dynamic_slice_in_dim(codebooks[1], lax.axis_index("tm") * part, part, axis=1)
    sums, squares, counts = main(
        latents,
        norm_gain,
        row_before,
        row_after,
        spatial_weight,
        temporal_weight,
        codebooks,
        table,
        got,
        slots,
        slabs,
        num_peers,
        capacity,
    )
    squares = jnp.sum(squares.reshape(slabs, total), axis=0)
    match = slots[1][:, None] == jnp.arange(total, dtype=jnp.int32)[None, :]
    error = jnp.sum(jnp.where(match, squares[None, :], 0.0), axis=1) / channels
    error = error.reshape(codes_first.shape)

    counts = counts.reshape(2, code_rows)
    keep = decay[:, None]
    wide = decay[:, None, None]
    ema_sums_new = wide * ema_sums + (1.0 - wide) * sums
    ema_counts_new = keep * ema_counts + (1.0 - keep) * counts
    return (ema_counts_new, ema_sums_new, error)


def solution(mesh):
    return jax.shard_map(
        body,
        mesh=mesh,
        in_specs=(
            P(None, "tm", "height", None, None),
            P(),
            P(),
            P(),
            P(None, "height", None),
            P(None, "height"),
            P(None, "height", "tm"),
            P(),
            P(None, "tm", "height", None),
            P(None, "tm", "height", None),
        ),
        out_specs=(P(None, "height"), P(None, "height", "tm"), P(None, "tm", "height", None)),
        check_vma=False,
    )
```

time: 214 us -> 203 us (0.949)
  Pallas kernels: 146 us -> 177 us
  matrix products: 15.4 us -> 0 us
  waiting for transfers between devices: 12.1 us -> 0.01 us
  starting transfers between devices: 11.4 us -> 3.71 us
  local copies, waits for them, and re-layouts: 11.3 us -> 4.49 us
    pallas_call x3 -> x1, Pallas kernels: 129 us -> 160 us  [main(): pl.pallas_call(kernel, out_shape=(jax.ShapeDtypeStruct((2, code_rows, par...]
    dot_general x2 -> x0, matrix products: 15.4 us -> none  [picked(): jnp.dot(rows_by(ids, table.shape[0]), table, preferred_element_type=jnp.f...]
    ppermute x1 -> x0, waiting for transfers between devices: 12.1 us -> none  [body(): earlier = lax.ppermute(hidden, 'tm', [(i, i + 1) for i in range(slabs - 1)])]
    reduce_sum x2 -> x0, other arithmetic: 6.77 us -> none  [body(): jnp.sum((marks == ids[None, :]).astype(jnp.float32), axis=1)]
    add x0 -> x1, other arithmetic: none -> 6.09 us  [body(): ema_sums_new = wide * ema_sums + (1.0 - wide) * sums]
    unnamed x23 -> x11, local copies, waits for them, and re-layouts: 6.84 us -> 0.84 us
    all_to_all x1 -> x0, starting transfers between devices: 4.92 us -> none  [body(): lax.all_to_all(answer, 'height', split_axis=0, concat_axis=0, tiled=True)]
    ppermute x1 -> x0, starting transfers between devices: 2.79 us -> none  [body(): earlier = lax.ppermute(hidden, 'tm', [(i, i + 1) for i in range(slabs - 1)])]
  transfers between devices with their start and end apart: 4 -> 2, of which waited for: 1 -> 0; matrix products, arithmetic and copies ran while one was open for 13% -> 2% of each run, Pallas kernels for 13% -> 8%
where the time goes in v3:
time: 203 us; the launch traced here: 202 us
  Pallas kernels  177 us (87%)
  other arithmetic  16.6 us (8%)
  local copies, waits for them, and re-layouts  4.49 us (2%)
  starting transfers between devices  3.71 us (2%)
    pallas_call x1, Pallas kernels, main(): pl.pallas_call(kernel, out_shape=(jax.ShapeDtypeStruct((2, code_rows, par...  160 us
    pallas_call x1, Pallas kernels, ask(): pl.pallas_call(kernel, out_shape=(jax.ShapeDtypeStruct(codes.shape, jnp.i...  16.9 us
    add x1, other arithmetic, body(): ema_sums_new = wide * ema_sums + (1.0 - wide) * sums  6.09 us
  transfers between devices with their start and end apart: 2, of which 0 were waited for; matrix products, arithmetic and copies ran while one was open for 2% of the time, Pallas kernels for 8%

profile of v3, /device:TPU:0, one launch (start us, length us, event | category | flops | bytes accessed | tf_op | source)
XLA Modules:
  0.0 202.4 jit_solution(16531902384029174491)
XLA Ops:
  0.6 0.0 slice-start
  0.6 1.6 fusion.3
  2.3 1.3 pad_add_fusion.code_ref
  3.6 2.3 %fusion.5 = (bf16[2,2,1,128,512]{4,3,2,1,0:T(8,128)(2,1)}, bf16[2,2,1,128,512]{4,3,2,1,0:T(8,128)(2,1)S(1)}) fusion(f32[2,2,128]{2,1,0:T(2,128)S(1)} %get-tuple-element.27, f32[512]{0:T(512)} %param.11, bf16[2,2,2,128,512]{4,3,2,1,0:T(8,128)(2,1)} %param.10, f32[2,2,128]{2,1,0:T(2,128)S(1)} %get-tuple-element.28), kind=kLoop, calls=%fused_computation.12 | loop fusion | flops 2097152 | bytes 2103296 | tf_op jit(solution)/shard_map/convert_element_type | solution.py:12
  5.9 2.4 %collective-permute-start = (bf16[2,2,1,128,512]{4,3,2,1,0:T(8,128)(2,1)}, bf16[2,2,1,128,512]{4,3,2,1,0:T(8,128)(2,1)S(1)}, u32[]{:S(2)}, u32[]{:S(2)}) collective-permute-start(bf16[2,2,1,128,512]{4,3,2,1,0:T(8,128)(2,1)} %get-tuple-element.11), channel_id=1, source_target_pairs={{0,1},{1,2},{2,3},{3,4},{4,5},{5,6},{6,7},{7,8},{8,9},{9,10},{10,1... | collective-permute-start | bytes 1572872 | tf_op jit(solution)/shard_map/ppermute | solution.py:473
  8.3 1.3 collective-permute-start.1
  9.6 16.9 %ask.1 = (s32[2,1024]{1,0:T(2,128)}, s32[32,2,128]{2,1,0:T(2,128)}) custom-call(s32[2,1024]{1,0:T(2,128)} %pad_add_fusion.code_ref), custom_call_target="tpu_custom_call" | custom-call | tf_op jit(solution)/shard_map/ask/pallas_call | solution.py:92
  26.6 0.0 copy-start.3
  26.6 1.5 slice_bitcast_fusion
  28.0 0.7 broadcast_subtract_fusion
  28.7 0.0 copy-done.3
  28.7 0.6 fusion.6
  29.3 0.0 slice-done
  29.3 1.0 dynamic-slice_bitcast_fusion.table_ref
  30.3 0.0 collective-permute-done
  30.4 0.0 copy-start
  30.4 0.0 collective-permute-done.1
  30.4 0.8 copy-done
  31.2 0.0 copy-start.1
  31.2 0.0 copy-start.4
  31.2 159.9 %main.1 = (f32[2,2048,256]{2,1,0:T(8,128)}, f32[32,1,128]{2,1,0:T(1,128)}, f32[2,8,1,256]{3,2,1,0:T(1,128)}) custom-call(bf16[4,256,512]{2,1,0:T(8,128)(2,1)} %bitcast.16, f32[1,512]{1,0:T(1,128)} %bitcast.21, bf16[4,128,512]{2,1,0:T(8,128)(2,1)} %bitcast.17, bf16[4,128,512]{2,1,0:T(8,128)(2,1)} %bitcast.5.after_ref, f32[3,512]{1,0:T(4,128)} %temporal_ref.1, ...), custom_call_target="tpu_custom_call" | custom-call | tf_op jit(solution)/shard_map/main/pallas_call | solution.py:398
  191.1 0.5 broadcast.59
  191.6 1.4 reduce.6
  193.0 0.0 copy-done.1
  193.1 1.2 select_reduce_fusion
  194.3 0.6 broadcast_multiply_fusion
  194.9 0.8 reduce.2
  195.6 0.0 copy-done.4
  195.6 0.0 copy-start.2
  195.7 6.1 %multiply_add_fusion = f32[2,2048,256]{2,1,0:T(8,128)} fusion(f32[2,2048,256]{2,1,0:T(8,128)} %get-tuple-element.17, f32[2,2048,256]{2,1,0:T(8,128)} %param.16, f32[2]{0:T(128)S(1)} %broadcast_subtract_fusion, f32[2]{0:T(128)S(1)} %copy-done.4), kind=kLoop, calls=%fused_computation.2 | loop fusion | flops 3145728 | bytes 12582928 | tf_op jit(solution)/shard_map/add | solution.py:501
  201.7 0.0 copy-done.2
  201.8 0.7 multiply_add_fusion.1
  (4 shorter events, 0.1 us)
Async XLA Ops:
  0.6 28.7 %slice-start = ((bf16[2,2048,512]{2,1,0:T(8,128)(2,1)}), bf16[1,2048,512]{2,1,0:T(8,128)(2,1)S(1)}, s32[]{:S(2)}) async-start(bf16[2,2048,512]{2,1,0:T(8,128)(2,1)} %book_hbm.1), calls=%async_computation | async-start | bytes 4194304 | tf_op jit(solution)/shard_map/slice | solution.py:477
  5.9 24.5 %collective-permute-start = (bf16[2,2,1,128,512]{4,3,2,1,0:T(8,128)(2,1)}, bf16[2,2,1,128,512]{4,3,2,1,0:T(8,128)(2,1)S(1)}, u32[]{:S(2)}, u32[]{:S(2)}) collective-permute-start(bf16[2,2,1,128,512]{4,3,2,1,0:T(8,128)(2,1)} %get-tuple-element.11), channel_id=1, source_target_pairs={{0,1},{1,2},{2,3},{3,4},{4,5},{5,6},{6,7},{7,8},{8,9},{9,10},{10,1... | collective-permute-start | bytes 1572872 | tf_op jit(solution)/shard_map/ppermute | solution.py:473
  8.3 22.0 %collective-permute-start.1 = (bf16[2,2,1,128,512]{4,3,2,1,0:T(8,128)(2,1)S(1)}, bf16[2,2,1,128,512]{4,3,2,1,0:T(8,128)(2,1)}, u32[]{:S(2)}, u32[]{:S(2)}) collective-permute-start(bf16[2,2,1,128,512]{4,3,2,1,0:T(8,128)(2,1)S(1)} %get-tuple-element.12), channel_id=1, source_target_pairs={{1,0},{2,1},{3,2},{4,3},{5,4},{6,5},{7,6},{8,7},{9,8},{10,9},{11,1... | collective-permute-start | bytes 1572872 | tf_op jit(solution)/shard_map/ppermute | solution.py:474
  26.6 2.1 %copy-start.3 = (s32[2,1024]{1,0:T(2,128)S(1)}, s32[2,1024]{1,0:T(2,128)}, u32[]{:S(2)}) copy-start(s32[2,1024]{1,0:T(2,128)} %get-tuple-element.15) | copy-start | bytes 24580
  30.4 0.8 copy-start
  31.2 161.9 %copy-start.1 = (s32[1,1024]{1,0:T(1,128)S(1)}, s32[1,1024]{1,0:T(1,128)}, u32[]{:S(2)}) copy-start(s32[1,1024]{1,0:T(1,128)} %get-tuple-element.25.second_slot_ref) | copy-start | bytes 12292
  31.2 164.5 %copy-start.4 = (f32[2]{0:T(128)S(1)}, f32[2]{0:T(128)}, u32[]{:S(2)}) copy-start(f32[2]{0:T(128)} %param.17) | copy-start | bytes 28
  195.6 6.1 %copy-start.2 = (f32[2,2048]{1,0:T(2,128)S(1)}, f32[2,2048]{1,0:T(2,128)}, u32[]{:S(2)}) copy-start(f32[2,2048]{1,0:T(2,128)} %param.15) | copy-start | bytes 49156

commit v4 on v3

--- a/solution.py
+++ b/solution.py
@@ -120,12 +120,9 @@
 def main(
     latents,
     norm_gain,
-    row_before,
-    row_after,
     spatial_weight,
     temporal_weight,
     codebooks,
-    table,
     got,
     slots,
     slabs,
@@ -150,21 +147,22 @@
     def kernel(
         latent_ref,
         gain_ref,
-        before_ref,
-        after_ref,
         temporal_ref,
-        table_ref,
         first_id_ref,
         second_id_ref,
         first_slot_ref,
         second_slot_ref,
         weight_hbm,
         book_hbm,
+        table_hbm,
         sums_ref,
         error_ref,
         count_ref,
         weight_ref,
         book_ref,
+        table_ref,
+        before_ref,
+        after_ref,
         served,
         answer,
         hidden,
@@ -187,8 +185,14 @@
         me = me_slab * num_peers + me_row
         load_book = pltpu.make_async_copy(book_hbm.at[0], book_ref, load_sems.at[0])
         load_weight = pltpu.make_async_copy(weight_hbm, weight_ref, load_sems.at[1])
+        wanted = table_hbm
+        if whole_table:
+            lanes = pl.ds(pl.multiple_of(me_slab * part, part), part)
+            wanted = table_hbm.at[1, :, lanes]
+        load_table = pltpu.make_async_copy(wanted, table_ref, load_sems.at[2])
         load_book.start()
         load_weight.start()
+        load_table.start()
 
         def peer_of(step):
             peer = lax.rem(me + step, members)
@@ -233,8 +237,33 @@
                 barrier, inc=1, device_id=target, device_id_type=pl.DeviceIdType.MESH
             )
 
+        @pl.when(me_row == 0)
+        def _():
+            before_ref[...] = jnp.zeros(before_ref.shape, jnp.bfloat16)
+
+        @pl.when(me_row == num_peers - 1)
+        def _():
+            after_ref[...] = jnp.zeros(after_ref.shape, jnp.bfloat16)
+
+        pl.semaphore_wait(barrier, members - 1)
+
+        def down():
+            target = {"tm": me_slab, "height": lax.rem(me_row + 1, num_peers)}
+            return push(latent_ref.at[:, pl.ds(pixels - width, width)], before_ref, 5, target)
+
+        def up():
+            target = {"tm": me_slab, "height": lax.rem(me_row + num_peers - 1, num_peers)}
+            return push(latent_ref.at[:, pl.ds(0, width)], after_ref, 6, target)
+
+        @pl.when(me_row < num_peers - 1)
+        def _():
+            down().start()
+
+        @pl.when(me_row > 0)
+        def _():
+            up().start()
+
         load_book.wait()
-        pl.semaphore_wait(barrier, members - 1)
 
         @pl.loop(0, num_peers // group)
         def _(step):
@@ -255,6 +284,17 @@
 
         own(served, answer, 3, me_row).start()
         load_weight.wait()
+
+        @pl.when(me_row < num_peers - 1)
+        def _():
+            down().wait_send()
+            up().wait_recv()
+
+        @pl.when(me_row > 0)
+        def _():
+            up().wait_send()
+            down().wait_recv()
+
         last_slab = me_slab + 1 >= slabs
         column = lax.rem(lax.broadcasted_iota(jnp.int32, (pixels, channels), 0), width)
 
@@ -268,8 +308,8 @@
 
         @pl.loop(0, images)
         def _(image):
-            normed = normalize(latent_ref[image], gain_ref[...])
-            taps = jnp.concatenate([before_ref[image], normed, after_ref[image]], axis=0)
+            taps = jnp.concatenate([before_ref[image], latent_ref[image], after_ref[image]], axis=0)
+            taps = normalize(taps, gain_ref[...])
             windows = [taps[row * width : (row + rows) * width] for row in range(3)]
 
             def tap(col):
@@ -288,6 +328,8 @@
             @pl.when(jnp.logical_not(last_slab))
             def _():
                 forward(image).start()
+
+        load_table.wait()
 
         @pl.loop(0, members // group)
         def _(step):
@@ -394,6 +436,11 @@
     vmem, anywhere = pl.BlockSpec(memory_space=pltpu.VMEM), pl.BlockSpec(memory_space=pl.ANY)
     bf16 = jnp.bfloat16
     pieces = (members, capacity, part)
+    whole_table = part % 128 == 0
+    table = codebooks
+    if not whole_table:
+        start = lax.axis_index("tm") * part
+        table = lax.dynamic_slice_in_dim(codebooks[1], start, part, axis=1)
     first_ids, second_ids = got[:, 0].reshape(-1), got[:, 1].reshape(-1)
     return pl.pallas_call(
         kernel,
@@ -402,11 +449,14 @@
             jax.ShapeDtypeStruct((members, 1, capacity), jnp.float32),
             jax.ShapeDtypeStruct((2, blocks, 1, block), jnp.float32),
         ),
-        in_specs=[vmem] * 10 + [anywhere] * 2,
+        in_specs=[vmem] * 7 + [anywhere] * 3,
         out_specs=(vmem, vmem, vmem),
         scratch_shapes=[
             pltpu.VMEM(spatial_weight.shape, bf16),
             pltpu.VMEM((code_rows, channels), bf16),
+            pltpu.VMEM((code_rows, part), bf16),
+            pltpu.VMEM((images, width, channels), bf16),
+            pltpu.VMEM((images, width, channels), bf16),
             pltpu.VMEM((num_peers, capacity, channels), bf16),
             pltpu.VMEM((num_peers, capacity, channels), bf16),
             pltpu.VMEM((images, pixels, channels), bf16),
@@ -419,10 +469,10 @@
             pltpu.VMEM(pieces, bf16),
             pltpu.VMEM(pieces, bf16),
             pltpu.VMEM((members, 1, capacity), jnp.float32),
-            pltpu.SemaphoreType.DMA((2,)),
+            pltpu.SemaphoreType.DMA((3,)),
             pltpu.SemaphoreType.DMA((4,)),
-            pltpu.SemaphoreType.DMA((5,)),
-            pltpu.SemaphoreType.DMA((5,)),
+            pltpu.SemaphoreType.DMA((7,)),
+            pltpu.SemaphoreType.DMA((7,)),
         ],
         compiler_params=pltpu.CompilerParams(
             collective_id=0, has_side_effects=True, vmem_limit_bytes=60 * 2**20
@@ -431,16 +481,14 @@
     )(
         latents.reshape(images, pixels, channels),
         norm_gain[None, :],
-        row_before.reshape(images, width, channels),
-        row_after.reshape(images, width, channels),
         temporal_weight,
-        table,
         first_ids[None, :],
         second_ids[None, :],
         slots[0][None, :],
         slots[1][None, :],
         spatial_weight,
         codebooks,
+        table,
     )
 
 
@@ -465,25 +513,14 @@
     capacity = 2 * amount // num_peers
     total = num_peers * capacity
 
-    peers = [(i, i + 1) for i in range(num_peers - 1)]
-    first_row = normalize(latents[:, :, :1], norm_gain)
-    last_row = normalize(latents[:, :, -1:], norm_gain)
     codes = jnp.stack([codes_first.reshape(-1), codes_second.reshape(-1)])
-    first_row, last_row, codes = lax.optimization_barrier((first_row, last_row, codes))
-    row_before = lax.ppermute(last_row, "height", peers)
-    row_after = lax.ppermute(first_row, "height", [(j, i) for i, j in peers])
-
     slots, got = ask(codes, num_peers, slabs, capacity, code_rows)
-    table = lax.dynamic_slice_in_dim(codebooks[1], lax.axis_index("tm") * part, part, axis=1)
     sums, squares, counts = main(
         latents,
         norm_gain,
-        row_before,
-        row_after,
         spatial_weight,
         temporal_weight,
         codebooks,
-        table,
         got,
         slots,
         slabs,

time: 203 us -> 193 us (0.951)
  other arithmetic: 16.6 us -> 11.4 us
  starting transfers between devices: 3.71 us -> 0 us
    pallas_call x1, Pallas kernels: 160 us -> 164 us  [main(): pl.pallas_call(kernel, out_shape=(jax.ShapeDtypeStruct((2, code_rows, par...]
    pallas_call x1, Pallas kernels: 16.9 us -> 12.9 us  [ask(): pl.pallas_call(kernel, out_shape=(jax.ShapeDtypeStruct(codes.shape, jnp.i...]
    ppermute x2 -> x0, starting transfers between devices: 3.71 us -> none  [the longest x1 2.42 us: body(): row_before = lax.ppermute(last_row, 'height', peers)]
    convert_element_type x1 -> x0, other arithmetic: 2.28 us -> none  [normalize(): return (widened * inverse * norm_gain).astype(jnp.bfloat16)]
  transfers between devices with their start and end apart: 2 -> 0, of which waited for: 0 -> 0; matrix products, arithmetic and copies ran while one was open for 2% -> 0% of each run, Pallas kernels for 8% -> 0%
where the time goes in v4:
time: 193 us
  Pallas kernels  177 us (92%)
  other arithmetic  11.4 us (6%)
  local copies, waits for them, and re-layouts  3.4 us (2%)
    pallas_call x1, Pallas kernels, main(): pl.pallas_call(kernel, out_shape=(jax.ShapeDtypeStruct((2, code_rows, par...  164 us
    pallas_call x1, Pallas kernels, ask(): pl.pallas_call(kernel, out_shape=(jax.ShapeDtypeStruct(codes.shape, jnp.i...  12.9 us
    add x1, other arithmetic, body(): ema_sums_new = wide * ema_sums + (1.0 - wide) * sums  6.1 us

profile of v4, /device:TPU:0, one launch (start us, length us, event | category | flops | bytes accessed | tf_op | source)
XLA Modules:
  0.0 192.7 jit_solution(6445517866184870909)
XLA Ops:
  0.6 1.3 pad_add_fusion.code_ref
  1.9 12.9 %ask.1 = (s32[2,1024]{1,0:T(2,128)}, s32[32,2,128]{2,1,0:T(2,128)}) custom-call(s32[2,1024]{1,0:T(2,128)} %pad_add_fusion.code_ref), custom_call_target="tpu_custom_call" | custom-call | tf_op jit(solution)/shard_map/ask/pallas_call | solution.py:92
  14.8 1.4 fusion
  16.2 1.5 slice_bitcast_fusion
  17.7 0.0 copy-start
  17.7 0.0 copy-start.3
  17.7 164.3 %main.1 = (f32[2,2048,256]{2,1,0:T(8,128)}, f32[32,1,128]{2,1,0:T(1,128)}, f32[2,8,1,256]{3,2,1,0:T(1,128)}) custom-call(bf16[4,256,512]{2,1,0:T(8,128)(2,1)} %bitcast.12, f32[1,512]{1,0:T(1,128)} %bitcast.19, f32[3,512]{1,0:T(4,128)} %temporal_ref.1, s32[1,4096]{1,0:T(1,128)} %get-tuple-element.14.first_id_ref, s32[1,4096]{1,0:T(1,128)} %get-tuple-element.13.second_id_ref, ...), custom_call_target="tpu_custom_call" | custom-call | tf_op jit(solution)/shard_map/main/pallas_call | solution.py:445
  182.0 0.5 broadcast.21
  182.5 1.4 reduce.4
  184.0 0.0 copy-done
  184.0 1.2 select_reduce_fusion
  185.2 0.6 broadcast_multiply_fusion
  185.8 0.0 copy-done.3
  185.8 0.0 copy-start.2
  185.8 0.0 copy-start.1
  185.8 6.1 %multiply_add_fusion = f32[2,2048,256]{2,1,0:T(8,128)} fusion(f32[2,2048,256]{2,1,0:T(8,128)} %get-tuple-element.11, f32[2,2048,256]{2,1,0:T(8,128)} %param.16, f32[2]{0:T(128)S(1)} %broadcast_subtract_fusion, f32[2]{0:T(128)S(1)} %copy-done.3), kind=kLoop, calls=%fused_computation.2 | loop fusion | flops 3145728 | bytes 12582928 | tf_op jit(solution)/shard_map/add | solution.py:538
  191.9 0.0 copy-done.2
  192.0 0.0 copy-done.1
  192.0 0.7 multiply_add_fusion.1
  (5 shorter events, 0.1 us)
Async XLA Ops:
  17.7 166.3 %copy-start = (s32[1,1024]{1,0:T(1,128)S(1)}, s32[1,1024]{1,0:T(1,128)}, u32[]{:S(2)}) copy-start(s32[1,1024]{1,0:T(1,128)} %get-tuple-element.15.second_slot_ref) | copy-start | bytes 12292
  17.7 168.1 %copy-start.3 = (f32[2]{0:T(128)S(1)}, f32[2]{0:T(128)}, u32[]{:S(2)}) copy-start(f32[2]{0:T(128)} %param.17) | copy-start | bytes 28
  185.8 6.1 %copy-start.2 = (f32[2,8,1,256]{3,2,1,0:T(1,128)S(1)}, f32[2,8,1,256]{3,2,1,0:T(1,128)}, u32[]{:S(2)}) copy-start(f32[2,8,1,256]{3,2,1,0:T(1,128)} %get-tuple-element.10) | copy-start | bytes 49156
  185.8 6.2 %copy-start.1 = (f32[2,2048]{1,0:T(2,128)S(1)}, f32[2,2048]{1,0:T(2,128)}, u32[]{:S(2)}) copy-start(f32[2,2048]{1,0:T(2,128)} %param.15) | copy-start | bytes 49156

commit v5 on v4

--- a/solution.py
+++ b/solution.py
@@ -139,6 +139,7 @@
     group = block_of(num_peers, 4)
     span = group * capacity
     pick_block = block_of(tokens, 256)
+    tally_block = block_of(code_rows, 256)
     block = code_rows
     while block * amount > 2**20 and block % 2 == 0:
         block //= 2
@@ -179,6 +180,7 @@
         local_sems,
         send_sems,
         recv_sems,
+        turn_sems,
     ):
         me_slab = lax.axis_index("tm")
         me_row = lax.axis_index("height")
@@ -382,21 +384,39 @@
             residual[here, :] = (flat[here, :].astype(jnp.float32) - quant).astype(jnp.bfloat16)
 
         pack(second_slot_ref, residual, second_out)
-        send(second_out, second_in, 1)
+
+        for turn in range(slabs):
+            slab = lax.rem(me_slab + turn, slabs)
+
+            @pl.loop(1 if turn == 0 else 0, num_peers)
+            def _(step):
+                row = lax.rem(me_row + step, num_peers)
+                pltpu.make_async_remote_copy(
+                    src_ref=second_out.at[slab * num_peers + row],
+                    dst_ref=second_in.at[me],
+                    send_sem=send_sems.at[1],
+                    recv_sem=turn_sems.at[turn],
+                    device_id={"tm": slab, "height": row},
+                    device_id_type=pl.DeviceIdType.MESH,
+                ).start()
+
         own(second_out, second_in, 1, me).start()
 
-        def tally(which, id_ref, landing, begin, end):
-            ids = id_ref[...]
+        def tally(which, id_ref, landing, turn, begin, end):
+            slab = lax.rem(me_slab + slabs - turn, slabs)
+            ids = id_ref[:, pl.ds(pl.multiple_of(slab * total, total), total)]
 
             @pl.loop(begin, end)
             def _(step):
-                start = pl.multiple_of(step * block, block)
-                places = start + lax.broadcasted_iota(jnp.int32, (block, amount), 0)
+                start = pl.multiple_of(step * tally_block, tally_block)
+                places = start + lax.broadcasted_iota(jnp.int32, (tally_block, total), 0)
                 hot = jnp.where(places == ids, 1.0, 0.0).astype(jnp.bfloat16)
-                vectors = landing[...].reshape(amount, part)
-                sums_ref[which, pl.ds(start, block), :] = jnp.dot(
-                    hot, vectors, preferred_element_type=jnp.float32
-                )
+                vectors = landing[pl.ds(slab * num_peers, num_peers)].reshape(total, part)
+                sums = jnp.dot(hot, vectors, preferred_element_type=jnp.float32)
+                here = pl.ds(start, tally_block)
+                if turn:
+                    sums = sums + sums_ref[which, here, :]
+                sums_ref[which, here, :] = sums
 
         for which, id_ref in ((0, first_id_ref), (1, second_id_ref)):
             ids = id_ref[...]
@@ -409,19 +429,33 @@
 
         own(first_out, first_in, 0, me).wait()
         finish(first_in, recv_sems, 0, members - 1)
-        tally(0, first_id_ref, first_in, 0, blocks)
+        tally_blocks = code_rows // tally_block
+        for turn in range(slabs):
+            tally(0, first_id_ref, first_in, turn, 0, tally_blocks)
         own(second_out, second_in, 1, me).wait()
-        finish(second_in, recv_sems, 1, members - 1)
-
-        @pl.loop(0, members)
-        def _(source):
-            leftover = second_in[source].astype(jnp.float32) - quants[source].astype(jnp.float32)
-            squares[source] = jnp.sum(leftover * leftover, axis=1)[None, :]
-
-        tally(1, second_id_ref, second_in, 0, 1)
-        send(squares, error_ref, 2)
-        own(squares, error_ref, 2, me).start()
-        tally(1, second_id_ref, second_in, 1, blocks)
+        for turn in range(slabs):
+            finish(second_in, turn_sems, turn, num_peers - (turn == 0))
+            slab = lax.rem(me_slab + slabs - turn, slabs)
+
+            @pl.loop(0, num_peers)
+            def _(row):
+                source = slab * num_peers + row
+                wide = second_in[source].astype(jnp.float32)
+                leftover = wide - quants[source].astype(jnp.float32)
+                squares[source] = jnp.sum(leftover * leftover, axis=1)[None, :]
+
+            tally(1, second_id_ref, second_in, turn, 0, 1)
+
+            @pl.loop(1 if turn == 0 else 0, num_peers)
+            def _(step):
+                row = lax.rem(me_row + step, num_peers)
+                target = {"tm": slab, "height": row}
+                push(squares.at[slab * num_peers + row], error_ref.at[me], 2, target).start()
+
+            if turn == 0:
+                own(squares, error_ref, 2, me).start()
+            tally(1, second_id_ref, second_in, turn, 1, tally_blocks)
+
         own(squares, error_ref, 2, me).wait()
         finish(error_ref, recv_sems, 2, members - 1)
         finish(first_in, send_sems, 0, members - 1)
@@ -473,6 +507,7 @@
             pltpu.SemaphoreType.DMA((4,)),
             pltpu.SemaphoreType.DMA((7,)),
             pltpu.SemaphoreType.DMA((7,)),
+            pltpu.SemaphoreType.DMA((slabs,)),
         ],
         compiler_params=pltpu.CompilerParams(
             collective_id=0, has_side_effects=True, vmem_limit_bytes=60 * 2**20

time: 193 us -> 191 us (0.990)
  Pallas kernels: 177 us -> 175 us
    pallas_call x1, Pallas kernels: 164 us -> 162 us  [main(): pl.pallas_call(kernel, out_shape=(jax.ShapeDtypeStruct((2, code_rows, par...]
where the time goes in v5:
time: 191 us; the launch traced here: 190 us
  Pallas kernels  175 us (92%)
  other arithmetic  11.4 us (6%)
  local copies, waits for them, and re-layouts  3.4 us (2%)
    pallas_call x1, Pallas kernels, main(): pl.pallas_call(kernel, out_shape=(jax.ShapeDtypeStruct((2, code_rows, par...  162 us
    pallas_call x1, Pallas kernels, ask(): pl.pallas_call(kernel, out_shape=(jax.ShapeDtypeStruct(codes.shape, jnp.i...  12.9 us
    add x1, other arithmetic, body(): ema_sums_new = wide * ema_sums + (1.0 - wide) * sums  6.1 us

profile of v5, /device:TPU:0, one launch (start us, length us, event | category | flops | bytes accessed | tf_op | source)
XLA Modules:
  0.0 190.2 jit_solution(15443936251199672457)
XLA Ops:
  0.6 1.3 pad_add_fusion.code_ref
  1.9 12.9 %ask.1 = (s32[2,1024]{1,0:T(2,128)}, s32[32,2,128]{2,1,0:T(2,128)}) custom-call(s32[2,1024]{1,0:T(2,128)} %pad_add_fusion.code_ref), custom_call_target="tpu_custom_call" | custom-call | tf_op jit(solution)/shard_map/ask/pallas_call | solution.py:92
  14.8 1.4 fusion
  16.2 1.5 slice_bitcast_fusion
  17.7 0.0 copy-start
  17.7 0.0 copy-start.3
  17.7 161.8 %main.1 = (f32[2,2048,256]{2,1,0:T(8,128)}, f32[32,1,128]{2,1,0:T(1,128)}, f32[2,8,1,256]{3,2,1,0:T(1,128)}) custom-call(bf16[4,256,512]{2,1,0:T(8,128)(2,1)} %bitcast.12, f32[1,512]{1,0:T(1,128)} %bitcast.19, f32[3,512]{1,0:T(4,128)} %temporal_ref.1, s32[1,4096]{1,0:T(1,128)} %get-tuple-element.14.first_id_ref, s32[1,4096]{1,0:T(1,128)} %get-tuple-element.13.second_id_ref, ...), custom_call_target="tpu_custom_call" | custom-call | tf_op jit(solution)/shard_map/main/pallas_call | solution.py:479
  179.5 0.5 broadcast.21
  180.1 1.4 reduce.4
  181.5 0.0 copy-done
  181.5 1.2 select_reduce_fusion
  182.7 0.6 broadcast_multiply_fusion
  183.3 0.0 copy-done.3
  183.3 0.0 copy-start.2
  183.3 0.0 copy-start.1
  183.3 6.1 %multiply_add_fusion = f32[2,2048,256]{2,1,0:T(8,128)} fusion(f32[2,2048,256]{2,1,0:T(8,128)} %get-tuple-element.11, f32[2,2048,256]{2,1,0:T(8,128)} %param.16, f32[2]{0:T(128)S(1)} %broadcast_subtract_fusion, f32[2]{0:T(128)S(1)} %copy-done.3), kind=kLoop, calls=%fused_computation.2 | loop fusion | flops 3145728 | bytes 12582928 | tf_op jit(solution)/shard_map/add | solution.py:573
  189.4 0.0 copy-done.2
  189.5 0.0 copy-done.1
  189.5 0.7 multiply_add_fusion.1
  (5 shorter events, 0.1 us)
Async XLA Ops:
  17.7 163.8 %copy-start = (s32[1,1024]{1,0:T(1,128)S(1)}, s32[1,1024]{1,0:T(1,128)}, u32[]{:S(2)}) copy-start(s32[1,1024]{1,0:T(1,128)} %get-tuple-element.15.second_slot_ref) | copy-start | bytes 12292
  17.7 165.6 %copy-start.3 = (f32[2]{0:T(128)S(1)}, f32[2]{0:T(128)}, u32[]{:S(2)}) copy-start(f32[2]{0:T(128)} %param.17) | copy-start | bytes 28
  183.3 6.1 %copy-start.2 = (f32[2,8,1,256]{3,2,1,0:T(1,128)S(1)}, f32[2,8,1,256]{3,2,1,0:T(1,128)}, u32[]{:S(2)}) copy-start(f32[2,8,1,256]{3,2,1,0:T(1,128)} %get-tuple-element.10) | copy-start | bytes 49156
  183.3 6.2 %copy-start.1 = (f32[2,2048]{1,0:T(2,128)S(1)}, f32[2,2048]{1,0:T(2,128)}, u32[]{:S(2)}) copy-start(f32[2,2048]{1,0:T(2,128)} %param.15) | copy-start | bytes 49156
